TPU v7x, 32 devices: a whole 2x2x4 slice. The times are simulated.
32 devices in a mesh: dp: 4 (over z), cent: 8 (over y, x, core).
Axes of the slice: x: 2, y: 2, z: 4, core: 2. Of those that a mesh axis runs over, the one named last changes fastest.
Arguments:
- vectors: bfloat16 [1024, 1024], P(('dp', 'cent')), may hold values from -18 to 18
- centroids: bfloat16 [16384, 1024], P('cent'), may hold values from -18 to 18
- primary: int32 [1024], P(('dp', 'cent')), may hold values from 0 to 16383, as said below
- secondary: int32 [1024], P(('dp', 'cent')), may hold values from 0 to 16383, as said below
Outputs:
- soft_cost: float32 [1024], P(('dp', 'cent'))
- list_sums: bfloat16 [16384, 1024], P('cent', 'dp')
Inputs may be any that keep to these rules, and one draw needn't show every extreme that they name: In each device's aligned block of 32 vectors at most 8 primary ids fall in one range of 2048 centroids (ids with equal id // 2048); in each dp group of 256 vectors one range receives exactly 8 from every block of the group. Secondary ids obey the same bound per block and range, and in each dp group the range that is full for primary ids is full for secondary ids too.
All inputs are finite; a program needn't handle non-finite values.
Results may differ from a plain program's by a relative error of at most 0.001.
Values may be sent and summed in bfloat16 or wider, within the bound.
No kernel may reach another device: no remote copies, remote signals or barrier semaphores. Data moves between devices by JAX's collectives and lax.ppermute only.
A program may use at most 64 MiB of HBM per device.

v0:
```python
import math

import jax
import jax.numpy as jnp
from jax import lax
from jax.sharding import PartitionSpec as P

perpendicular_weighting = 1.5
logit_divisor = 40.0
spill_offset = 2.0
block_rows = 512


def merged(array, axis, combine):
    everything = jax.tree.map(lambda part: lax.all_gather(part, axis), array)
    initial = jax.tree.map(lambda part: part[0], everything)

    def hop(k, so_far):
        return combine(so_far, jax.tree.map(lambda part: part[k], everything))

    return lax.fori_loop(1, lax.axis_size(axis), hop, initial)


def score_block(block_x, block_r, sec_local, centroids, center_length_squared):
    x_float = block_x.astype(jnp.float32)
    r_float = block_r.astype(jnp.float32)
    leftover_dot_point = jnp.sum(r_float * x_float, axis=1)
    logit_range_gap = jnp.mean(r_float * r_float, axis=1) + 1e-05
    piece_rows = block_x.shape[0]
    feature_width = block_x.shape[1]
    stacked = jnp.concatenate([block_x, block_r], axis=0)
    products = lax.dot_general(
        stacked, centroids, (((1,), (1,)), ((), ())), preferred_element_type=jnp.float32
    )
    normalized_exponent_likelihood = (
        2.0 * products[:piece_rows]
        - center_length_squared[None, :]
        - perpendicular_weighting
        * (leftover_dot_point[:, None] - products[piece_rows:]) ** 2
        / (feature_width * logit_range_gap[:, None])
    ) / logit_divisor
    row_top = jnp.max(normalized_exponent_likelihood, axis=1)
    row_total = jnp.sum(jnp.exp(normalized_exponent_likelihood - row_top[:, None]), axis=1)
    columns = lax.broadcasted_iota(jnp.int32, normalized_exponent_likelihood.shape, 1)
    picked = jnp.sum(
        jnp.where(columns == sec_local[:, None], normalized_exponent_likelihood, 0.0), axis=1
    )
    return (row_top, row_total, picked)


def combine_parts(first, second):
    row_top = jnp.maximum(first[0], second[0])
    return (
        row_top,
        first[1] * jnp.exp(first[0] - row_top) + second[1] * jnp.exp(second[0] - row_top),
    )


def per_device(vectors, centroids, primary, secondary):
    row_count, feature_width = vectors.shape
    cent_rows = centroids.shape[0]
    cent_devices = lax.axis_size("cent")
    dp_devices = lax.axis_size("dp")
    group_size = row_count * cent_devices
    offset = lax.axis_index("cent") * cent_rows
    prim_group, sec_group = (
        lax.all_gather(primary, "cent", axis=0, tiled=True),
        lax.all_gather(secondary, "cent", axis=0, tiled=True),
    )
    local_group = prim_group - offset
    inside_group = (local_group >= 0) & (local_group < cent_rows)
    found_rows = jnp.take(
        centroids,
        jnp.where(inside_group, local_group, cent_rows),
        axis=0,
        mode="fill",
        fill_value=0,
    )
    primary_rows = (
        lax.psum_scatter(found_rows, "cent", scatter_dimension=0, tiled=True)
        .astype(jnp.float32)
        .astype(jnp.bfloat16)
    )
    residual = (vectors.astype(jnp.float32) - primary_rows.astype(jnp.float32)).astype(jnp.bfloat16)
    cent_float = centroids.astype(jnp.float32)
    center_length_squared = jnp.sum(cent_float * cent_float, axis=1)
    sec_shifted = sec_group - offset
    piece_x = lax.all_gather(vectors, "cent", axis=0, tiled=True)
    piece_r = lax.all_gather(residual, "cent", axis=0, tiled=True)
    piece_rows = piece_x.shape[0]
    if piece_rows > block_rows and piece_rows % block_rows == 0:
        block_count = piece_rows // block_rows

        def one_block(packed):
            return score_block(packed[0], packed[1], packed[2], centroids, center_length_squared)

        row_top, row_total, picked = lax.map(
            one_block,
            (
                piece_x.reshape(block_count, block_rows, feature_width),
                piece_r.reshape(block_count, block_rows, feature_width),
                sec_shifted.reshape(block_count, block_rows),
            ),
        )
        row_top = row_top.reshape(piece_rows)
        row_total = row_total.reshape(piece_rows)
        picked = picked.reshape(piece_rows)
    else:
        row_top, row_total, picked = score_block(
            piece_x, piece_r, sec_shifted, centroids, center_length_squared
        )
    group_x = piece_x
    row_tops = row_top
    totals = row_total
    row_picks = picked
    group_x, row_tops, totals, row_picks = (group_x, row_tops, totals, row_picks)
    row_tops, totals = merged((row_tops, totals), "cent", combine_parts)
    lse = row_tops + jnp.log(totals)
    log_count = math.log(cent_rows * cent_devices)
    own_lse = lax.dynamic_slice_in_dim(lse, lax.axis_index("cent") * row_count, row_count)
    soft_cost = own_lse - log_count
    spill_weight = jax.nn.sigmoid(row_picks - lse + log_count + spill_offset)
    list_ids = jnp.concatenate([prim_group, sec_group]) - offset
    weights = jnp.concatenate([jnp.ones((group_size,), jnp.float32), spill_weight])
    inside = (list_ids >= 0) & (list_ids < cent_rows)
    doubled_x = jnp.concatenate([group_x, group_x], axis=0)
    slot_total = 4 * row_count
    candidates = 2 * group_size
    slot_place = jnp.cumsum(inside.astype(jnp.int32)) - 1
    slot_place = jnp.where(inside, slot_place, slot_total)
    chosen = (
        jnp.full((slot_total,), candidates, jnp.int32)
        .at[slot_place]
        .set(jnp.arange(candidates, dtype=jnp.int32), mode="drop")
    )
    slot_valid = chosen < candidates
    slot_pick = jnp.minimum(chosen, candidates - 1)
    slot_ids = jnp.where(slot_valid, list_ids[slot_pick], cent_rows)
    slot_weight = jnp.where(slot_valid, weights[slot_pick], 0.0)
    list_terms = slot_weight[:, None] * (
        doubled_x[slot_pick].astype(jnp.float32)
        - jnp.take(centroids, slot_ids, axis=0, mode="fill", fill_value=0).astype(jnp.float32)
    )
    slot_tags = jnp.broadcast_to(slot_ids[:, None], (slot_total, dp_devices))
    got_rows, got_tags = (
        lax.all_to_all(list_terms, "dp", split_axis=1, concat_axis=0, tiled=True),
        lax.all_to_all(slot_tags, "dp", split_axis=1, concat_axis=0, tiled=True),
    )
    list_part = (
        jnp.zeros((cent_rows, feature_width // dp_devices), jnp.float32)
        .at[got_tags[:, 0]]
        .add(got_rows, mode="drop")
    )
    return (soft_cost, list_part.astype(jnp.bfloat16))


def solution(mesh):
    in_specs = (P(("dp", "cent"), None), P("cent", None), P(("dp", "cent")), P(("dp", "cent")))
    out_specs = (P(("dp", "cent")), P("cent", "dp"))
    return jax.shard_map(
        per_device, mesh=mesh, in_specs=in_specs, out_specs=out_specs, check_vma=False
    )
```

profile of v0, /device:TPU:0, one launch (start us, length us, event | category | flops | bytes accessed | tf_op | source)
XLA Modules:
  0.0 127.7 jit_solution(1731169717444635222)
XLA Ops:
  7.2 0.0 reduce-scatter.2.cloned.1.call-start
  7.2 1.2 dynamic-slice
  9.1 0.9 dynamic-update-slice
  10.0 0.8 dynamic-update-slice.1
  10.8 9.5 %all-reduce.3 = (s32[256]{0:T(256)S(1)}, s32[256]{0:T(256)S(1)}) all-reduce(s32[256]{0:T(256)S(1)} %dynamic-update-slice, s32[256]{0:T(256)S(1)} %dynamic-update-slice.1), channel_id=1, replica_groups=mesh['dp'=4,'cent'=8] {'cent'}, use_global_device_ids=true, to_apply=%add.1 | all-reduce | flops 512 | bytes 4096
  20.3 4.3 %gather_fusion = bf16[256,1024]{1,0:T(8,128)(2,1)S(1)} fusion(bf16[2048,1024]{1,0:T(8,128)(2,1)} %param.7, s32[1024]{0:T(1024)S(1)} %pad_clamp_fusion.2), kind=kCustom, calls=%fused_computation | custom fusion | bytes 1049600 | tf_op jit(solution)/shard_map/jit(_take)/gather | solution.py:72
  24.6 0.0 copy-start
  24.6 0.9 broadcast_select_fusion
  25.5 0.0 reduce-scatter.2.cloned.1.call-update
  25.6 0.3 reduce-window.9
  25.9 0.1 slice.23
  26.0 0.1 slice_reduce_fusion
  26.1 0.1 add_add_fusion
  26.2 2.4 %scatter_custom_fusion = s32[128]{0:T(128)S(1)} fusion(s32[512]{0:T(512)S(1)} %bitcast.59, s32[512]{0:T(512)S(1)} %iota.8, s32[]{:T(128)} %constant.114.clone.1), kind=kCustom, calls=%fused_computation.64 | custom fusion | bytes 516 | tf_op jit(solution)/shard_map/scatter | solution.py:134
  28.7 1.3 gather_fusion.1
  30.0 0.6 broadcast_in_dim.71
  30.6 4.9 %all-to-all-start = ((s32[128,4,1]{0,2,1:T(1,128)}), s32[128,4,1]{0,2,1:T(1,128)S(1)}, u32[]{:S(2)}, u32[]{:S(2)}) async-start(s32[128,4,1]{0,2,1:T(1,128)} %broadcast_in_dim.71), calls=%async_computation.1 | async-start | bytes 4096 | tf_op jit(solution)/shard_map/all_to_all | solution.py:147
  35.4 0.0 copy-done
  35.4 9.2 %all_gather.24 = bf16[256,1024]{1,0:T(8,128)(2,1)S(1)} all-gather(bf16[32,1024]{1,0:T(8,128)(2,1)S(1)} %copy-done), channel_id=1, replica_groups=mesh['dp'=4,'cent'=8] {'cent'}, dimensions={0}, use_global_device_ids=true | all-gather | bytes 589824 | tf_op jit(solution)/shard_map/all_gather | solution.py:88
  44.6 3.8 %gather_fusion.4 = bf16[128,1024]{1,0:T(8,128)(2,1)S(1)} fusion(bf16[2048,1024]{1,0:T(8,128)(2,1)} %param.7, s32[1024]{0:T(1024)S(1)} %pad_clamp_fusion), kind=kCustom, calls=%fused_computation.4 | custom fusion | bytes 524800 | tf_op jit(solution)/shard_map/jit(_take)/gather | solution.py:142
  48.4 0.1 pad_maximum_fusion
  48.6 0.9 gather_fusion.3
  49.5 3.1 %multiply_reduce_fusion = f32[2048]{0:T(1024)S(1)} fusion(bf16[2048,1024]{1,0:T(8,128)(2,1)} %param.7), kind=kLoop, calls=%fused_computation.10 | loop fusion | flops 6289408 | bytes 4202496 | tf_op jit(solution)/shard_map/reduce_sum | solution.py:86
  52.6 6.9 %reduce-scatter.2.cloned.1.call-done = bf16[32,1024]{1,0:T(8,128)(2,1)} async-done(((bf16[256,1024]{1,0:T(8,128)(2,1)}), bf16[32,1024]{1,0:T(8,128)(2,1)}) %reduce-scatter.2.cloned.1.call-update) | async-done | bytes 65552 | tf_op jit(solution)/shard_map/reduce_scatter | solution.py:80
  59.5 0.9 subtract_convert_fusion
  60.4 9.8 %all_gather.26 = bf16[256,1024]{1,0:T(8,128)(2,1)S(1)} all-gather(bf16[32,1024]{1,0:T(8,128)(2,1)S(1)} %subtract_convert_fusion), channel_id=1, replica_groups=mesh['dp'=4,'cent'=8] {'cent'}, dimensions={0}, use_global_device_ids=true | all-gather | bytes 589824 | tf_op jit(solution)/shard_map/all_gather | solution.py:89
  70.2 0.3 fusion.7
  70.4 4.6 %fusion.6 = f32[512,2048]{1,0:T(8,128)S(1)} fusion(bf16[2048,1024]{1,0:T(8,128)(2,1)} %param.7, bf16[256,1024]{1,0:T(8,128)(2,1)S(1)} %all_gather.24, bf16[256,1024]{1,0:T(8,128)(2,1)S(1)} %all_gather.26), kind=kOutput, calls=%fused_computation.26 | convolution fusion | flops 2149580800 | bytes 9437184 | tf_op jit(solution)/shard_map/dot_general | solution.py:32
  75.0 0.8 fusion.16
  75.8 0.8 select_reduce_fusion
  76.6 8.2 %all-gather.3 = f32[8,1,256]{2,1,0:T(1,128)S(1)} all-gather(f32[1,1,256]{2,1,0:T(1,128)S(1)} %bitcast.57), channel_id=3, replica_groups=mesh['dp'=4,'cent'=8] {'cent'}, dimensions={0}, use_global_device_ids=true | all-gather | bytes 9216 | tf_op jit(solution)/shard_map/all_gather | solution.py:15
  84.8 8.9 %all-gather.2 = f32[8,1,256]{2,1,0:T(1,128)S(1)} all-gather(f32[1,1,256]{2,1,0:T(1,128)S(1)} %bitcast.55), channel_id=2, replica_groups=mesh['dp'=4,'cent'=8] {'cent'}, dimensions={0}, use_global_device_ids=true | all-gather | bytes 9216 | tf_op jit(solution)/shard_map/all_gather | solution.py:15
  93.6 0.4 while.17
  94.0 1.3 gather_fusion.2
  95.3 1.0 fusion.12
  96.3 0.0 all-to-all-done
  96.3 4.6 %all-to-all-start.1 = ((f32[128,4,256]{2,0,1:T(8,128)}), f32[128,4,256]{2,0,1:T(8,128)S(1)}, u32[]{:S(2)}, u32[]{:S(2)}) async-start(f32[128,4,256]{2,0,1:T(8,128)} %fusion.12), calls=%async_computation.2 | async-start | bytes 1048576 | tf_op jit(solution)/shard_map/all_to_all | solution.py:146
  100.9 0.6 dynamic-slice_add_fusion
  101.5 14.4 %all-to-all-done.1 = f32[128,4,256]{2,0,1:T(8,128)S(1)} async-done(((f32[128,4,256]{2,0,1:T(8,128)}), f32[128,4,256]{2,0,1:T(8,128)S(1)}, u32[]{:S(2)}, u32[]{:S(2)}) %all-to-all-start.1) | async-done | bytes 524320 | tf_op jit(solution)/shard_map/all_to_all | solution.py:146
  115.9 3.8 %scatter_custom_fusion.1 = f32[2048,256]{1,0:T(8,128)S(1)} fusion(s32[512]{0:T(512)S(1)} %bitcast.58, f32[512,256]{1,0:T(8,128)S(1)} %bitcast.44, f32[]{:T(128)} %constant.104.clone.1), kind=kCustom, calls=%fused_computation.30 | custom fusion | flops 131072 | bytes 2097156 | tf_op jit(solution)/shard_map/scatter-add | solution.py:152
  119.7 1.1 convert_element_type.48
  (39 shorter events, 0.4 us)
Async XLA Ops:
  7.2 52.3 %reduce-scatter.2.cloned.1.call-start = ((), (), s32[]{:S(2)}) async-start(), calls=%async_computation.3 | async-start | bytes 589824 | tf_op jit(solution)/shard_map/reduce_scatter | solution.py:80
  24.6 10.8 %copy-start = (bf16[32,1024]{1,0:T(8,128)(2,1)S(1)}, bf16[32,1024]{1,0:T(8,128)(2,1)}, u32[]{:S(2)}) copy-start(bf16[32,1024]{1,0:T(8,128)(2,1)} %param.6) | copy-start | bytes 196612
  30.6 65.7 %all-to-all-start = ((s32[128,4,1]{0,2,1:T(1,128)}), s32[128,4,1]{0,2,1:T(1,128)S(1)}, u32[]{:S(2)}, u32[]{:S(2)}) async-start(s32[128,4,1]{0,2,1:T(1,128)} %broadcast_in_dim.71), calls=%async_computation.1 | async-start | bytes 4096 | tf_op jit(solution)/shard_map/all_to_all | solution.py:147
  96.3 19.6 %all-to-all-start.1 = ((f32[128,4,256]{2,0,1:T(8,128)}), f32[128,4,256]{2,0,1:T(8,128)S(1)}, u32[]{:S(2)}, u32[]{:S(2)}) async-start(f32[128,4,256]{2,0,1:T(8,128)} %fusion.12), calls=%async_computation.2 | async-start | bytes 1048576 | tf_op jit(solution)/shard_map/all_to_all | solution.py:146
Sparse Core Ops, SparseCore 0:
  25.7 33.7 reduce-scatter.1
where the time goes:
time: 128 us
  blocking collectives  45.5 us (36%)
  waiting for transfers between devices  21.4 us (17%)
  local copies, waits for them, and re-layouts  17.7 us (14%)
  between operations  14.9 us (12%)
  other arithmetic  14 us (11%)
  starting transfers between devices  9.53 us (7%)
  matrix products  4.55 us (4%)
    all_gather x2, blocking collectives, merged(): everything = jax.tree.map(lambda part: lax.all_gather(part, axis), array)  17 us
    all_to_all x1, waiting for transfers between devices, per_device(): lax.all_to_all(list_terms, 'dp', split_axis=1, concat_axis=0, tiled=True)  14.4 us
    all_gather x1, blocking collectives, per_device(): piece_r = lax.all_gather(residual, 'cent', axis=0, tiled=True)  9.79 us
    unnamed x1, blocking collectives  9.49 us
    all_gather x1, blocking collectives, per_device(): piece_x = lax.all_gather(vectors, 'cent', axis=0, tiled=True)  9.2 us
    reduce_scatter x1, waiting for transfers between devices, per_device(): lax.psum_scatter(found_rows, 'cent', scatter_dimension=0, tiled=True)  6.93 us
    all_to_all x1, starting transfers between devices, per_device(): lax.all_to_all(slot_tags, 'dp', split_axis=1, concat_axis=0, tiled=True)  4.87 us
    all_to_all x1, starting transfers between devices, per_device(): lax.all_to_all(list_terms, 'dp', split_axis=1, concat_axis=0, tiled=True)  4.62 us
  transfers between devices with their start and end apart: 3, of which 2 were waited for; matrix products, arithmetic and copies ran while one was open for 18% of the time, Pallas kernels for 0%

commit v1 on v0

v1 whole, which is shorter than its diff:
```python
import functools
import math

import jax
import jax.numpy as jnp
from jax import lax
from jax.experimental import pallas as pl
from jax.experimental.pallas import tpu as pltpu
from jax.sharding import PartitionSpec as P

perpendicular_weighting = 1.5
logit_divisor = 40.0
spill_offset = 2.0
BF = jnp.bfloat16
F32 = jnp.float32
I32 = jnp.int32
META = 8
VMEM_LIMIT = 24 * 1024 * 1024


def iota(shape, dim):
    return lax.broadcasted_iota(I32, shape, dim)


def nn(a, b):
    return lax.dot_general(a, b, (((1,), (0,)), ((), ())), preferred_element_type=F32)


def nt(a, b):
    return lax.dot_general(a, b, (((1,), (1,)), ((), ())), preferred_element_type=F32)


def as_bf(mask):
    return jnp.where(mask, 1.0, 0.0).astype(BF)


def call(kernel, outs, args, flops=0, nbytes=0, scratch=(), smem=0, limit=VMEM_LIMIT):
    specs = [pl.BlockSpec(memory_space=pltpu.SMEM)] * smem
    specs += [pl.BlockSpec(memory_space=pltpu.VMEM)] * (len(args) - smem)
    return pl.pallas_call(
        kernel,
        out_shape=tuple(jax.ShapeDtypeStruct(s, t) for s, t in outs),
        in_specs=specs,
        out_specs=tuple(pl.BlockSpec(memory_space=pltpu.VMEM) for _ in outs),
        scratch_shapes=list(scratch),
        compiler_params=pltpu.CompilerParams(vmem_limit_bytes=limit),
        cost_estimate=pl.CostEstimate(flops=flops, bytes_accessed=nbytes, transcendentals=0),
    )(*args)


def pack_kernel(x_ref, prim_ref, sec_ref, out_ref):
    rows = x_ref.shape[0]
    out_ref[0:rows, :] = x_ref[...]
    out_ref[rows:, 0:128] = jnp.zeros((META, 128), BF)
    for q, ref in ((0, prim_ref), (2, sec_ref)):
        ids = ref[...]
        out_ref[rows + q : rows + q + 1, 0:rows] = (ids >> 8).astype(F32).astype(BF)
        out_ref[rows + q + 1 : rows + q + 2, 0:rows] = (ids & 255).astype(F32).astype(BF)


def rows_kernel(rows, cap, parts, shift, me_ref, *refs):
    blocks = refs[:parts]
    cent_ref, info_ref, out_ref = refs[parts:]
    group = rows * parts
    me = me_ref[0]
    spread = as_bf(iota((128, group), 0) == (iota((128, group), 1) % rows))
    lane_block = iota((META, group), 1) // rows
    bytes8 = jnp.zeros((META, group), F32)
    for s, ref in enumerate(blocks):
        got = nn(ref[rows : rows + META, 0:128], spread)
        bytes8 = bytes8 + jnp.where(lane_block == (me ^ s), got, 0.0)
    bytes8 = bytes8.astype(I32)
    prim = bytes8[0:1] * 256 + bytes8[1:2]
    sec = bytes8[2:3] * 256 + bytes8[3:4]
    before = (iota((group, group), 0) < iota((group, group), 1)) & (
        iota((group, group), 0) // rows == iota((group, group), 1) // rows
    )
    before = as_bf(before)
    ranks = []
    for ids in (prim, sec):
        same = iota((parts, group), 0) == (ids >> shift)
        count = nn(as_bf(same), before)
        ranks.append(jnp.sum(jnp.where(same, count, 0.0), axis=0, keepdims=True).astype(I32))
    base = (iota((1, group), 1) // rows) * cap
    slot_p = base + ranks[0]
    slot_s = base + ranks[1]
    info_ref[0:1, :] = prim
    info_ref[1:2, :] = sec
    info_ref[2:3, :] = slot_p
    info_ref[3:4, :] = slot_s
    info_ref[4:8, :] = jnp.zeros((4, group), I32)
    slots = cap * parts
    keep = (iota((slots, group), 0) == slot_p) & ((prim >> shift) == me)
    local = jnp.where(keep, (prim & ((1 << shift) - 1)) + 1, 0).astype(F32)
    row_id = jnp.sum(local, axis=1, keepdims=True).astype(I32) - 1
    pick = as_bf(iota((slots, 1 << shift), 1) == row_id)
    out_ref[...] = nn(pick, cent_ref[...]).astype(BF)


def slots_kernel(rows, cap, parts, dps, shift, me_ref, *refs):
    blocks = refs[:parts]
    info_ref, x_ref = refs[parts : parts + 2]
    outs = refs[parts + 2 : parts + 2 + dps]
    picked_ref = refs[-1]
    group = rows * parts
    slots = cap * parts
    me = me_ref[0]
    me_dp = me_ref[1]
    for s, ref in enumerate(blocks):
        at = pl.multiple_of((me ^ s) * rows, rows)
        x_ref[pl.ds(at, rows), :] = ref[0:rows, :]
    prim, sec = info_ref[0:1, :], info_ref[1:2, :]
    slot_p, slot_s = info_ref[2:3, :], info_ref[3:4, :]
    keep_p = (iota((slots, group), 0) == slot_p) & ((prim >> shift) == me)
    keep_s = (iota((slots, group), 0) == slot_s) & ((sec >> shift) == me)
    pick = jnp.concatenate([as_bf(keep_p), as_bf(keep_s)], axis=0)
    picked_ref[...] = nn(pick, x_ref[...]).astype(BF)
    where = iota((1, group), 1)
    meta = jnp.concatenate(
        [
            jnp.ones((1, group), F32),
            (where >> 8).astype(F32),
            (where & 255).astype(F32),
            jnp.zeros((5, group), F32),
        ],
        axis=0,
    ).astype(BF)
    mask = (1 << shift) - 1
    local_p, local_s = prim & mask, sec & mask
    loc = jnp.concatenate(
        [
            (local_p >> 8).astype(F32),
            (local_p & 255).astype(F32),
            (local_s >> 8).astype(F32),
            (local_s & 255).astype(F32),
            jnp.zeros((4, group), F32),
        ],
        axis=0,
    ).astype(BF)
    facts = jnp.concatenate([nt(meta, pick), nt(loc, pick)], axis=0).astype(BF)
    width = x_ref.shape[1] // dps
    for s in range(dps):
        at = pl.multiple_of((me_dp ^ s) * width, width)
        outs[s][0 : 2 * slots, :] = picked_ref[:, pl.ds(at, width)]
        outs[s][2 * slots :, 0:128] = facts


def base_kernel(tile, x_ref, cent_ref, out_ref):
    x = x_ref[...]

    @pl.loop(0, cent_ref.shape[0], step=tile)
    def _(k):
        k = pl.multiple_of(k, tile)
        c = cent_ref[pl.ds(k, tile), :]
        cf = c.astype(F32)
        norm = jnp.sum(cf * cf, axis=1, keepdims=True)
        out_ref[pl.ds(k, tile), :] = 2.0 * nt(c, x) - norm


def score_kernel(rows, cap, parts, shift, tile, me_ref, *refs):
    owned = refs[:parts]
    x_ref, info_ref, cent_ref, base_ref, out_ref, r_ref, t_ref = refs[parts:]
    group = rows * parts
    slots = cap * parts
    me = me_ref[0]
    dim = x_ref.shape[1]
    prim, sec, slot_p = info_ref[0:1, :], info_ref[1:2, :], info_ref[2:3, :]
    place = ((prim >> shift) ^ me) * slots + slot_p
    place = jnp.transpose(jnp.broadcast_to(place.astype(F32), (128, group)))[:, 0:1].astype(I32)
    pick = as_bf(iota((group, parts * slots), 1) == place)
    found = nn(pick, jnp.concatenate([ref[...] for ref in owned], axis=0))
    x = x_ref[...]
    r_ref[...] = (x.astype(F32) - found).astype(BF)
    r = r_ref[...]
    diag = iota((group, group), 0) == iota((group, group), 1)
    rx = jnp.sum(jnp.where(diag, nt(x, r), 0.0), axis=0, keepdims=True)
    rr = jnp.sum(jnp.where(diag, nt(r, r), 0.0), axis=0, keepdims=True)
    spread = rr * (1.0 / dim) + 1e-05
    gain = perpendicular_weighting / (dim * spread)
    sec_row = jnp.where((sec >> shift) == me, sec & ((1 << shift) - 1), -1)

    def first(i, so_far):
        top, picked = so_far
        k = pl.multiple_of(i * tile, tile)
        gap = rx - nt(cent_ref[pl.ds(k, tile), :], r)
        t = (base_ref[pl.ds(k, tile), :] - gain * (gap * gap)) * (1.0 / logit_divisor)
        t_ref[pl.ds(k, tile), :] = t
        hit = (iota((tile, group), 0) + k) == sec_row
        picked = picked + jnp.sum(jnp.where(hit, t, 0.0), axis=0, keepdims=True)
        return jnp.maximum(top, jnp.max(t, axis=0, keepdims=True)), picked

    count = cent_ref.shape[0] // tile
    top, picked = lax.fori_loop(
        0, count, first, (jnp.full((1, group), -jnp.inf, F32), jnp.zeros((1, group), F32))
    )

    def second(i, total):
        k = pl.multiple_of(i * tile, tile)
        e = jnp.exp(t_ref[pl.ds(k, tile), :] - top)
        return total + jnp.sum(e, axis=0, keepdims=True)

    total = lax.fori_loop(0, count, second, jnp.zeros((1, group), F32))
    part = top + jnp.log(total)
    lines = [part[:, i : i + 128] for i in range(0, group, 128)]
    lines += [picked[:, i : i + 128] for i in range(0, group, 128)]
    packed = jnp.concatenate(lines, axis=0)
    out_ref[...] = jnp.broadcast_to(packed[None], out_ref.shape)


def three(a):
    high = a.astype(BF)
    rest = a - high.astype(F32)
    mid = rest.astype(BF)
    return [high, mid, (rest - mid.astype(F32)).astype(BF)]


def lists_kernel(cap, parts, dps, shift, group, tile, me_ref, *refs):
    blocks = refs[:dps]
    cent_ref, sum_ref, diff_ref, hot_ref, lane_ref = refs[dps:]
    slots = cap * parts
    cents = 1 << shift
    width = blocks[0].shape[1]
    at = pl.multiple_of(me_ref[1] * width, width)
    diffs = []
    for s, ref in enumerate(blocks):
        facts = ref[2 * slots :, 0:128].astype(F32)
        valid = facts[0:1, :] > 0.0
        second = iota((1, 128), 1) >= slots
        high = jnp.where(second, facts[10:11, :], facts[8:9, :])
        low = jnp.where(second, facts[11:12, :], facts[9:10, :])
        ids = jnp.where(valid, high * 256.0 + low, -1.0)
        where = jnp.where(valid, facts[1:2, :] * 256.0 + facts[2:3, :], -1.0)
        hot_ref[:, s * 128 : (s + 1) * 128] = as_bf(iota((cents, 128), 0) == ids.astype(I32))
        ids_col = jnp.transpose(jnp.broadcast_to(ids, (128, 128)))[:, 0:1].astype(I32)
        where_col = jnp.transpose(jnp.broadcast_to(where, (128, 128)))[slots:, 0:1].astype(I32)
        lane_ref[s * slots : (s + 1) * slots, :] = jnp.where(
            iota((slots, group), 1) == where_col, 1.0, 0.0
        )
        pick = as_bf(iota((128, cents), 1) == ids_col)
        rows = nn(pick, cent_ref[:, pl.ds(at, width)])
        diff = ref[0 : 2 * slots, :].astype(F32) - rows
        diff_ref[s * slots : (s + 1) * slots, :] = diff[slots:, :]
        diffs.append(jnp.concatenate([diff[0:slots, :], jnp.zeros((slots, width), F32)], axis=0))
    parts3 = three(jnp.concatenate(diffs, axis=0))

    @pl.loop(0, cents, step=tile)
    def _(k):
        k = pl.multiple_of(k, tile)
        hot = hot_ref[pl.ds(k, tile), :]
        sum_ref[pl.ds(k, tile), :] = nn(hot, parts3[0]) + nn(hot, parts3[1]) + nn(hot, parts3[2])


def final_kernel(rows, cap, parts, dps, group, tile, log_count, me_ref, *refs):
    got_ref, sum_ref, diff_ref, hot_ref, lane_ref, cost_ref, out_ref = refs
    slots = cap * parts
    lines = group // 128
    me = me_ref[0]
    terms = []
    for s in range(dps):
        first = (me_ref[1] ^ s) * parts
        part = got_ref[pl.ds(first, parts), 0:lines, :]
        top = jnp.max(part, axis=0)
        lse = top + jnp.log(jnp.sum(jnp.exp(part - top[None]), axis=0))
        if s == 0:
            flat = jnp.concatenate([lse[i : i + 1] for i in range(lines)], axis=1)
            cost = jnp.zeros((1, rows), F32)
            for b in range(parts):
                cost = cost + jnp.where(me == b, flat[:, b * rows : (b + 1) * rows], 0.0)
            cost_ref[...] = cost - log_count
        picked = got_ref[pl.ds(first + me, 1), lines : 2 * lines, :][0]
        z = picked - lse + log_count + spill_offset
        e = jnp.exp(-jnp.abs(z))
        weight = jnp.where(z >= 0.0, 1.0, e) / (1.0 + e)
        weight = jnp.concatenate([weight[i : i + 1] for i in range(lines)], axis=1)
        at = slice(s * slots, (s + 1) * slots)
        column = jnp.sum(lane_ref[at, :] * weight, axis=1, keepdims=True)
        terms.append(jnp.zeros((slots, diff_ref.shape[1]), F32))
        terms.append(column * diff_ref[at, :])
    parts3 = three(jnp.concatenate(terms, axis=0))

    @pl.loop(0, out_ref.shape[0], step=tile)
    def _(k):
        k = pl.multiple_of(k, tile)
        hot = hot_ref[pl.ds(k, tile), :]
        late = nn(hot, parts3[0]) + nn(hot, parts3[1]) + nn(hot, parts3[2])
        out_ref[pl.ds(k, tile), :] = (sum_ref[pl.ds(k, tile), :] + late).astype(BF)


def swap(a, axis, count, step):
    return lax.ppermute(a, axis, [(i, i ^ step) for i in range(count)])


def exchange(a, axis, count):
    blocks = [None] * count
    for s in range(0, count, 2):
        blocks[s] = swap(a, axis, count, s) if s else a
    for s in range(0, count, 2):
        blocks[s + 1] = swap(blocks[s], axis, count, 1)
    return blocks


def per_device(vectors, centroids, primary, secondary):
    rows, dim = vectors.shape
    cents = centroids.shape[0]
    parts = lax.axis_size("cent")
    dps = lax.axis_size("dp")
    group = rows * parts
    cap = 2 * rows // parts
    slots = cap * parts
    shift = cents.bit_length() - 1
    assert cents == 1 << shift and 2 * slots == 128
    width = dim // dps
    tile = 256
    me = jnp.stack([lax.axis_index("cent"), lax.axis_index("dp")]).astype(I32)

    (packed,) = call(
        pack_kernel,
        [((rows + META, dim), BF)],
        [vectors, primary.reshape(1, rows), secondary.reshape(1, rows)],
    )
    blocks = exchange(packed, "cent", parts)
    info, owned = call(
        functools.partial(rows_kernel, rows, cap, parts, shift),
        [((8, group), I32), ((slots, dim), BF)],
        [me, *blocks, centroids],
        smem=1,
    )
    owned = exchange(owned, "cent", parts)
    x_all, *columns = call(
        functools.partial(slots_kernel, rows, cap, parts, dps, shift),
        [((group, dim), BF)] + [((2 * slots + 16, width), BF)] * dps,
        [me, *blocks, info],
        smem=1,
        scratch=[pltpu.VMEM((2 * slots, dim), BF)],
    )
    columns = [columns[0]] + [swap(columns[s], "dp", dps, s) for s in range(1, dps)]
    (base,) = call(
        functools.partial(base_kernel, tile),
        [((cents, group), F32)],
        [x_all, centroids],
    )
    lines = group // 128
    (sent,) = call(
        functools.partial(score_kernel, rows, cap, parts, shift, tile),
        [((dps * parts, 2 * lines, 128), F32)],
        [me, *owned, x_all, info, centroids, base],
        smem=1,
        scratch=[pltpu.VMEM((group, dim), BF), pltpu.VMEM((cents, group), F32)],
        limit=40 * 1024 * 1024,
    )
    got = lax.all_to_all(sent, ("dp", "cent"), 0, 0, tiled=True)
    list_sum, diff, hot, lane = call(
        functools.partial(lists_kernel, cap, parts, dps, shift, group, tile),
        [
            ((cents, width), F32),
            ((dps * slots, width), F32),
            ((cents, dps * 2 * slots), BF),
            ((dps * slots, group), F32),
        ],
        [me, *columns, centroids],
        smem=1,
    )
    log_count = math.log(cents * parts)
    cost, out = call(
        functools.partial(final_kernel, rows, cap, parts, dps, group, tile, log_count),
        [((1, rows), F32), ((cents, width), BF)],
        [me, got, list_sum, diff, hot, lane],
        smem=1,
    )
    return cost.reshape(rows), out


def solution(mesh):
    in_specs = (P(("dp", "cent"), None), P("cent", None), P(("dp", "cent")), P(("dp", "cent")))
    out_specs = (P(("dp", "cent")), P("cent", "dp"))
    return jax.shard_map(
        per_device, mesh=mesh, in_specs=in_specs, out_specs=out_specs, check_vma=False
    )
```

time: 128 us -> 67.8 us (0.53)
  blocking collectives: 45.5 us -> 0 us
  Pallas kernels: 0 us -> 21.2 us
  between operations: 14.9 us -> 0.74 us
  other arithmetic: 14 us -> 0.07 us
  starting transfers between devices: 9.53 us -> 18 us
  local copies, waits for them, and re-layouts: 17.7 us -> 9.46 us
  matrix products: 4.55 us -> 0 us
  waiting for transfers between devices: 21.4 us -> 17.9 us
    all_gather x4 -> x0, blocking collectives: 36 us -> none  [the longest x2 17 us: merged(): everything = jax.tree.map(lambda part: lax.all_gather(part, axis), array)]
    pallas_call x0 -> x7, Pallas kernels: none -> 21.2 us  [call(): pl.pallas_call(kernel, out_shape=tuple((jax.ShapeDtypeStruct(s, t) for s,...]
    ppermute x0 -> x17, waiting for transfers between devices: none -> 17.9 us  [swap(): return lax.ppermute(a, axis, [(i, i ^ step) for i in range(count)])]
    all_to_all x2 -> x1, waiting for transfers between devices: 14.4 us -> 0.01 us  [per_device(): got = lax.all_to_all(sent, ('dp', 'cent'), 0, 0, tiled=True)]
    ppermute x0 -> x17, starting transfers between devices: none -> 13.1 us  [swap(): return lax.ppermute(a, axis, [(i, i ^ step) for i in range(count)])]
    gather x5 -> x0, local copies, waits for them, and re-layouts: 11.5 us -> none  [the longest x1 4.29 us: per_device(): jnp.take(centroids, jnp.where(inside_group, local_group, cent_rows), axis...]
    unnamed x1 -> x0, blocking collectives: 9.49 us -> none
    reduce_scatter x1 -> x0, waiting for transfers between devices: 6.93 us -> none  [per_device(): lax.psum_scatter(found_rows, 'cent', scatter_dimension=0, tiled=True)]
  transfers between devices with their start and end apart: 3 -> 18, of which waited for: 2 -> 10; matrix products, arithmetic and copies ran while one was open for 18% -> 0% of each run, Pallas kernels for 0% -> 14%
where the time goes in v1:
time: 67.8 us; the launch traced here: 67.5 us
  Pallas kernels  21.2 us (31%)
  starting transfers between devices  18 us (27%)
  waiting for transfers between devices  17.9 us (26%)
  local copies, waits for them, and re-layouts  9.46 us (14%)
  between operations  0.74 us (1%)
    pallas_call x7, Pallas kernels, call(): pl.pallas_call(kernel, out_shape=tuple((jax.ShapeDtypeStruct(s, t) for s,...  21.2 us
    ppermute x17, waiting for transfers between devices, swap(): return lax.ppermute(a, axis, [(i, i ^ step) for i in range(count)])  17.9 us
    ppermute x17, starting transfers between devices, swap(): return lax.ppermute(a, axis, [(i, i ^ step) for i in range(count)])  13.1 us
    unnamed x16, local copies, waits for them, and re-layouts  9.46 us
    all_to_all x1, starting transfers between devices, per_device(): got = lax.all_to_all(sent, ('dp', 'cent'), 0, 0, tiled=True)  4.95 us
  transfers between devices with their start and end apart: 18, of which 10 were waited for; matrix products, arithmetic and copies ran while one was open for 0% of the time, Pallas kernels for 14%

profile of v1, /device:TPU:0, one launch (start us, length us, event | category | flops | bytes accessed | tf_op | source)
XLA Modules:
  0.0 67.5 jit_solution(1339586124195416946)
XLA Ops:
  0.6 0.0 copy-start.5
  0.6 0.8 %copy-done.5 = bf16[32,1024]{1,0:T(8,128)(2,1)S(1)} copy-done((bf16[32,1024]{1,0:T(8,128)(2,1)S(1)}, bf16[32,1024]{1,0:T(8,128)(2,1)}, u32[]{:S(2)}) %copy-start.5) | copy-done | bytes 65560
  1.5 0.0 copy-start.6
  1.5 0.7 copy-done.6
  2.1 0.0 copy-start.7
  2.1 0.7 copy-done.7
  2.8 4.0 %collective-permute-start.5 = (bf16[40,1024]{1,0:T(8,128)(2,1)S(1)}, bf16[40,1024]{1,0:T(8,128)(2,1)S(1)}, u32[]{:S(2)}, u32[]{:S(2)}) collective-permute-start(bf16[40,1024]{1,0:T(8,128)(2,1)S(1)} %shard_map.59.refs_0_), channel_id=1, source_target_pairs={{0,6},{1,7},{2,4},{3,5},{4,2},{5,3},{6,0},{7,1},{8,14},{9,15},{10,... | collective-permute-start | bytes 245768 | tf_op jit(solution)/shard_map/ppermute | solution.py:290
  6.8 0.5 collective-permute-start.3
  7.3 0.1 collective-permute-start.1
  7.4 0.0 collective-permute-start
  7.4 1.9 %collective-permute-done.5.refs_6_ = bf16[40,1024]{1,0:T(8,128)(2,1)S(1)} collective-permute-done((bf16[40,1024]{1,0:T(8,128)(2,1)S(1)}, bf16[40,1024]{1,0:T(8,128)(2,1)S(1)}, u32[]{:S(2)}, u32[]{:S(2)}) %collective-permute-start.5) | collective-permute-done | bytes 81952 | tf_op jit(solution)/shard_map/ppermute | solution.py:290
  9.4 0.0 collective-permute-start.6
  9.4 1.9 %collective-permute-done.3.refs_4_ = bf16[40,1024]{1,0:T(8,128)(2,1)S(1)} collective-permute-done((bf16[40,1024]{1,0:T(8,128)(2,1)S(1)}, bf16[40,1024]{1,0:T(8,128)(2,1)S(1)}, u32[]{:S(2)}, u32[]{:S(2)}) %collective-permute-start.3) | collective-permute-done | bytes 81952 | tf_op jit(solution)/shard_map/ppermute | solution.py:290
  11.2 0.0 collective-permute-start.4
  11.2 0.5 collective-permute-done.1.refs_2_
  11.7 0.0 collective-permute-start.2
  11.7 0.1 pad_add_fusion.me_ref
  11.8 0.0 collective-permute-done.refs_1_
  11.8 0.0 collective-permute-done.6.refs_7_
  11.8 0.7 %collective-permute-done.4.refs_5_ = bf16[40,1024]{1,0:T(8,128)(2,1)S(1)} collective-permute-done((bf16[40,1024]{1,0:T(8,128)(2,1)S(1)}, bf16[40,1024]{1,0:T(8,128)(2,1)S(1)}, u32[]{:S(2)}, u32[]{:S(2)}) %collective-permute-start.4) | collective-permute-done | bytes 81952 | tf_op jit(solution)/shard_map/ppermute | solution.py:290
  12.5 0.5 collective-permute-done.2.refs_3_
  13.0 0.0 copy-start
  13.0 2.2 %copy-done = bf16[2048,1024]{1,0:T(8,128)(2,1)S(1)} copy-done((bf16[2048,1024]{1,0:T(8,128)(2,1)S(1)}, bf16[2048,1024]{1,0:T(8,128)(2,1)}, u32[]{:S(2)}) %copy-start) | copy-done | bytes 4194328
  15.2 0.0 copy-start.1
  15.2 1.7 %shard_map.60 = (s32[8,256]{1,0:T(8,128)S(1)}, bf16[64,1024]{1,0:T(8,128)(2,1)S(1)}) custom-call(s32[2]{0:T(128)S(1)} %pad_add_fusion.me_ref, bf16[40,1024]{1,0:T(8,128)(2,1)S(1)} %shard_map.59.refs_0_, bf16[40,1024]{1,0:T(8,128)(2,1)S(1)} %collective-permute-done.refs_1_, bf16[40,1024]{1,0:T(8,128)(2,1)S(1)} %collective-permute-done.1.refs_2_, ...), custom_call_target="tpu_custom_call" | custom-call | tf_op jit(solution)/shard_map/pallas_call | solution.py:40
  16.9 1.6 %collective-permute-start.12 = (bf16[64,1024]{1,0:T(8,128)(2,1)S(1)}, bf16[64,1024]{1,0:T(8,128)(2,1)S(1)}, u32[]{:S(2)}, u32[]{:S(2)}) collective-permute-start(bf16[64,1024]{1,0:T(8,128)(2,1)S(1)} %get-tuple-element.15.refs_0_), channel_id=1, source_target_pairs={{0,6},{1,7},{2,4},{3,5},{4,2},{5,3},{6,0},{7,1},{8,14},{9,15},{10,... | collective-permute-start | bytes 393224 | tf_op jit(solution)/shard_map/ppermute | solution.py:290
  18.5 1.0 %collective-permute-start.10 = (bf16[64,1024]{1,0:T(8,128)(2,1)S(1)}, bf16[64,1024]{1,0:T(8,128)(2,1)S(1)}, u32[]{:S(2)}, u32[]{:S(2)}) collective-permute-start(bf16[64,1024]{1,0:T(8,128)(2,1)S(1)} %get-tuple-element.15.refs_0_), channel_id=1, source_target_pairs={{0,4},{1,5},{2,6},{3,7},{4,0},{5,1},{6,2},{7,3},{8,12},{9,13},{10,... | collective-permute-start | bytes 393224 | tf_op jit(solution)/shard_map/ppermute | solution.py:290
  19.6 0.9 %collective-permute-start.8 = (bf16[64,1024]{1,0:T(8,128)(2,1)S(1)}, bf16[64,1024]{1,0:T(8,128)(2,1)S(1)}, u32[]{:S(2)}, u32[]{:S(2)}) collective-permute-start(bf16[64,1024]{1,0:T(8,128)(2,1)S(1)} %get-tuple-element.15.refs_0_), channel_id=1, source_target_pairs={{0,2},{1,3},{2,0},{3,1},{4,6},{5,7},{6,4},{7,5},{8,10},{9,11},{10,... | collective-permute-start | bytes 393224 | tf_op jit(solution)/shard_map/ppermute | solution.py:290
  20.5 0.0 collective-permute-start.7
  20.5 3.8 %collective-permute-done.12.refs_6_ = bf16[64,1024]{1,0:T(8,128)(2,1)S(1)} collective-permute-done((bf16[64,1024]{1,0:T(8,128)(2,1)S(1)}, bf16[64,1024]{1,0:T(8,128)(2,1)S(1)}, u32[]{:S(2)}, u32[]{:S(2)}) %collective-permute-start.12) | collective-permute-done | bytes 131104 | tf_op jit(solution)/shard_map/ppermute | solution.py:290
  24.3 0.0 collective-permute-start.13
  24.3 2.0 %collective-permute-done.10.refs_4_ = bf16[64,1024]{1,0:T(8,128)(2,1)S(1)} collective-permute-done((bf16[64,1024]{1,0:T(8,128)(2,1)S(1)}, bf16[64,1024]{1,0:T(8,128)(2,1)S(1)}, u32[]{:S(2)}, u32[]{:S(2)}) %collective-permute-start.10) | collective-permute-done | bytes 131104 | tf_op jit(solution)/shard_map/ppermute | solution.py:290
  26.3 0.0 collective-permute-start.11
  26.3 0.1 collective-permute-done.8.refs_2_
  26.4 0.4 collective-permute-start.9
  26.8 0.9 %shard_map.61 = (bf16[256,1024]{1,0:T(8,128)(2,1)S(1)}, bf16[144,256]{1,0:T(8,128)(2,1)S(1)}, bf16[144,256]{1,0:T(8,128)(2,1)S(1)}, bf16[144,256]{1,0:T(8,128)(2,1)S(1)}, bf16[144,256]{1,0:T(8,128)(2,1)S(1)}) custom-call(s32[2]{0:T(128)S(1)} %pad_add_fusion.me_ref, bf16[40,1024]{1,0:T(8,128)(2,1)S(1)} %shard_map.59.refs_0_, ...), custom_call_target="tpu_custom_call" | custom-call | tf_op jit(solution)/shard_map/pallas_call | solution.py:40
  27.7 0.0 copy-done.1
  27.7 3.1 %shard_map.62.refs_11_ = f32[2048,256]{1,0:T(8,128)S(1)} custom-call(bf16[256,1024]{1,0:T(8,128)(2,1)S(1)} %get-tuple-element.17.x_ref.refs_8_, bf16[2048,1024]{1,0:T(8,128)(2,1)S(1)} %copy-done.1), custom_call_target="tpu_custom_call" | custom-call | tf_op jit(solution)/shard_map/pallas_call | solution.py:40
  30.7 0.0 collective-permute-done.7.refs_1_
  30.8 0.0 collective-permute-done.13.refs_7_
  30.8 0.0 collective-permute-done.11.refs_5_
  30.8 0.0 collective-permute-done.9.refs_3_
  30.8 5.5 %shard_map.63 = f32[32,4,128]{2,1,0:T(4,128)} custom-call(s32[2]{0:T(128)S(1)} %pad_add_fusion.me_ref, bf16[64,1024]{1,0:T(8,128)(2,1)S(1)} %get-tuple-element.15.refs_0_, bf16[64,1024]{1,0:T(8,128)(2,1)S(1)} %collective-permute-done.7.refs_1_, bf16[64,1024]{1,0:T(8,128)(2,1)S(1)} %collective-permute-done.8.refs_2_, ...), custom_call_target="tpu_custom_call" | custom-call | tf_op jit(solution)/shard_map/pallas_call | solution.py:40
  36.3 5.0 %all-to-all-start = ((f32[32,4,128]{2,1,0:T(4,128)}), f32[32,4,128]{2,1,0:T(4,128)S(1)}, u32[]{:S(2)}, u32[]{:S(2)}) async-start(f32[32,4,128]{2,1,0:T(4,128)} %shard_map.63), calls=%async_computation | async-start | bytes 131072 | tf_op jit(solution)/shard_map/all_to_all | solution.py:351
  41.3 1.8 %collective-permute-start.14 = (bf16[144,256]{1,0:T(8,128)(2,1)S(1)}, bf16[144,256]{1,0:T(8,128)(2,1)S(1)}, u32[]{:S(2)}, u32[]{:S(2)}) collective-permute-start(bf16[144,256]{1,0:T(8,128)(2,1)S(1)} %get-tuple-element.19), channel_id=1, source_target_pairs={{0,8},{8,0},{16,24},{24,16},{1,9},{9,1},{17,25},{25,17},{2,10},{10... | collective-permute-start | bytes 221192 | tf_op jit(solution)/shard_map/ppermute | solution.py:290
  43.1 2.4 %collective-permute-start.15 = (bf16[144,256]{1,0:T(8,128)(2,1)S(1)}, bf16[144,256]{1,0:T(8,128)(2,1)S(1)}, u32[]{:S(2)}, u32[]{:S(2)}) collective-permute-start(bf16[144,256]{1,0:T(8,128)(2,1)S(1)} %get-tuple-element.20), channel_id=1, source_target_pairs={{0,16},{8,24},{16,0},{24,8},{1,17},{9,25},{17,1},{25,9},{2,18},{10... | collective-permute-start | bytes 221192 | tf_op jit(solution)/shard_map/ppermute | solution.py:290
  45.5 0.2 collective-permute-start.16
  45.7 1.3 %collective-permute-done.14.refs_1_ = bf16[144,256]{1,0:T(8,128)(2,1)S(1)} collective-permute-done((bf16[144,256]{1,0:T(8,128)(2,1)S(1)}, bf16[144,256]{1,0:T(8,128)(2,1)S(1)}, u32[]{:S(2)}, u32[]{:S(2)}) %collective-permute-start.14) | collective-permute-done | bytes 73760 | tf_op jit(solution)/shard_map/ppermute | solution.py:290
  47.1 5.2 %collective-permute-done.15.refs_2_ = bf16[144,256]{1,0:T(8,128)(2,1)S(1)} collective-permute-done((bf16[144,256]{1,0:T(8,128)(2,1)S(1)}, bf16[144,256]{1,0:T(8,128)(2,1)S(1)}, u32[]{:S(2)}, u32[]{:S(2)}) %collective-permute-start.15) | collective-permute-done | bytes 73760 | tf_op jit(solution)/shard_map/ppermute | solution.py:290
  52.3 0.0 collective-permute-done.16.refs_3_
  52.3 0.0 copy-start.2
  52.3 2.2 %copy-done.2 = bf16[2048,1024]{1,0:T(8,128)(2,1)S(1)} copy-done((bf16[2048,1024]{1,0:T(8,128)(2,1)S(1)}, bf16[2048,1024]{1,0:T(8,128)(2,1)}, u32[]{:S(2)}) %copy-start.2) | copy-done | bytes 4194328
  54.5 5.3 %shard_map.64 = (f32[2048,256]{1,0:T(8,128)S(1)}, f32[256,256]{1,0:T(8,128)S(1)}, bf16[2048,512]{1,0:T(8,128)(2,1)S(1)}, f32[256,256]{1,0:T(8,128)S(1)}) custom-call(s32[2]{0:T(128)S(1)} %pad_add_fusion.me_ref, bf16[144,256]{1,0:T(8,128)(2,1)S(1)} %get-tuple-element.18.refs_0_, bf16[144,256]{1,0:T(8,128)(2,1)S(1)} %collective-permute-done.14.refs_1_, ...), custom_call_target="tpu_custom_call" | custom-call | tf_op jit(solution)/shard_map/pallas_call | solution.py:40
  59.8 0.0 copy-start.3
  59.8 1.3 %copy-done.3 = bf16[2048,512]{1,0:T(8,128)(2,1)} copy-done((bf16[2048,512]{1,0:T(8,128)(2,1)}, bf16[2048,512]{1,0:T(8,128)(2,1)S(1)}, u32[]{:S(2)}) %copy-start.3) | copy-done | bytes 2097176
  61.1 0.0 all-to-all-done.refs_0_
  61.1 0.0 copy-start.4
  61.1 1.6 %copy-done.4 = bf16[2048,512]{1,0:T(8,128)(2,1)S(1)} copy-done((bf16[2048,512]{1,0:T(8,128)(2,1)S(1)}, bf16[2048,512]{1,0:T(8,128)(2,1)}, u32[]{:S(2)}) %copy-start.4) | copy-done | bytes 2097176
  62.7 4.7 %shard_map.65 = (f32[1,32]{1,0:T(1,128)}, bf16[2048,256]{1,0:T(8,128)(2,1)}) custom-call(s32[2]{0:T(128)S(1)} %pad_add_fusion.me_ref, f32[32,4,128]{2,1,0:T(4,128)S(1)} %all-to-all-done.refs_0_, f32[2048,256]{1,0:T(8,128)S(1)} %get-tuple-element.22.refs_1_, f32[256,256]{1,0:T(8,128)S(1)} %get-tuple-element.23.refs_2_, bf16[2048,512]{1,0:T(8,128)(2,1)S(1)} %copy-done.4, ...), custom_call_target="tpu_custom_call" | custom-call | tf_op jit(solution)/shard_map/pallas_call | solution.py:40
  (1 shorter events, 0.0 us)
Async XLA Ops:
  0.6 0.8 %copy-start.5 = (bf16[32,1024]{1,0:T(8,128)(2,1)S(1)}, bf16[32,1024]{1,0:T(8,128)(2,1)}, u32[]{:S(2)}) copy-start(bf16[32,1024]{1,0:T(8,128)(2,1)} %x_ref.1) | copy-start | bytes 196612
  1.5 0.7 copy-start.6
  2.1 0.7 copy-start.7
  2.8 6.6 %collective-permute-start.5 = (bf16[40,1024]{1,0:T(8,128)(2,1)S(1)}, bf16[40,1024]{1,0:T(8,128)(2,1)S(1)}, u32[]{:S(2)}, u32[]{:S(2)}) collective-permute-start(bf16[40,1024]{1,0:T(8,128)(2,1)S(1)} %shard_map.59.refs_0_), channel_id=1, source_target_pairs={{0,6},{1,7},{2,4},{3,5},{4,2},{5,3},{6,0},{7,1},{8,14},{9,15},{10,... | collective-permute-start | bytes 245768 | tf_op jit(solution)/shard_map/ppermute | solution.py:290
  6.8 4.4 %collective-permute-start.3 = (bf16[40,1024]{1,0:T(8,128)(2,1)S(1)}, bf16[40,1024]{1,0:T(8,128)(2,1)S(1)}, u32[]{:S(2)}, u32[]{:S(2)}) collective-permute-start(bf16[40,1024]{1,0:T(8,128)(2,1)S(1)} %shard_map.59.refs_0_), channel_id=1, source_target_pairs={{0,4},{1,5},{2,6},{3,7},{4,0},{5,1},{6,2},{7,3},{8,12},{9,13},{10,... | collective-permute-start | bytes 245768 | tf_op jit(solution)/shard_map/ppermute | solution.py:290
  7.3 4.4 %collective-permute-start.1 = (bf16[40,1024]{1,0:T(8,128)(2,1)S(1)}, bf16[40,1024]{1,0:T(8,128)(2,1)S(1)}, u32[]{:S(2)}, u32[]{:S(2)}) collective-permute-start(bf16[40,1024]{1,0:T(8,128)(2,1)S(1)} %shard_map.59.refs_0_), channel_id=1, source_target_pairs={{0,2},{1,3},{2,0},{3,1},{4,6},{5,7},{6,4},{7,5},{8,10},{9,11},{10,... | collective-permute-start | bytes 245768 | tf_op jit(solution)/shard_map/ppermute | solution.py:290
  7.4 4.4 %collective-permute-start = (bf16[40,1024]{1,0:T(8,128)(2,1)S(1)}, bf16[40,1024]{1,0:T(8,128)(2,1)S(1)}, u32[]{:S(2)}, u32[]{:S(2)}) collective-permute-start(bf16[40,1024]{1,0:T(8,128)(2,1)S(1)} %shard_map.59.refs_0_), channel_id=1, source_target_pairs={{0,1},{1,0},{2,3},{3,2},{4,5},{5,4},{6,7},{7,6},{8,9},{9,8},{10,11... | collective-permute-start | bytes 245768 | tf_op jit(solution)/shard_map/ppermute | solution.py:290
  9.4 2.5 %collective-permute-start.6 = (bf16[40,1024]{1,0:T(8,128)(2,1)S(1)}, bf16[40,1024]{1,0:T(8,128)(2,1)S(1)}, u32[]{:S(2)}, u32[]{:S(2)}) collective-permute-start(bf16[40,1024]{1,0:T(8,128)(2,1)S(1)} %collective-permute-done.5.refs_6_), channel_id=1, source_target_pairs={{0,1},{1,0},{2,3},{3,2},{4,5},{5,4},{6,7},{7,6},{8,9},{9,8},{10,11... | collective-permute-start | bytes 245768 | tf_op jit(solution)/shard_map/ppermute | solution.py:290
  11.2 1.3 %collective-permute-start.4 = (bf16[40,1024]{1,0:T(8,128)(2,1)S(1)}, bf16[40,1024]{1,0:T(8,128)(2,1)S(1)}, u32[]{:S(2)}, u32[]{:S(2)}) collective-permute-start(bf16[40,1024]{1,0:T(8,128)(2,1)S(1)} %collective-permute-done.3.refs_4_), channel_id=1, source_target_pairs={{0,1},{1,0},{2,3},{3,2},{4,5},{5,4},{6,7},{7,6},{8,9},{9,8},{10,11... | collective-permute-start | bytes 245768 | tf_op jit(solution)/shard_map/ppermute | solution.py:290
  11.7 1.3 %collective-permute-start.2 = (bf16[40,1024]{1,0:T(8,128)(2,1)S(1)}, bf16[40,1024]{1,0:T(8,128)(2,1)S(1)}, u32[]{:S(2)}, u32[]{:S(2)}) collective-permute-start(bf16[40,1024]{1,0:T(8,128)(2,1)S(1)} %collective-permute-done.1.refs_2_), channel_id=1, source_target_pairs={{0,1},{1,0},{2,3},{3,2},{4,5},{5,4},{6,7},{7,6},{8,9},{9,8},{10,11... | collective-permute-start | bytes 245768 | tf_op jit(solution)/shard_map/ppermute | solution.py:290
  13.0 2.2 %copy-start = (bf16[2048,1024]{1,0:T(8,128)(2,1)S(1)}, bf16[2048,1024]{1,0:T(8,128)(2,1)}, u32[]{:S(2)}) copy-start(bf16[2048,1024]{1,0:T(8,128)(2,1)} %refs_4_.1) | copy-start | bytes 12582916
  15.2 12.5 %copy-start.1 = (bf16[2048,1024]{1,0:T(8,128)(2,1)S(1)}, bf16[2048,1024]{1,0:T(8,128)(2,1)}, u32[]{:S(2)}) copy-start(bf16[2048,1024]{1,0:T(8,128)(2,1)} %refs_4_.1) | copy-start | bytes 12582916
  16.9 7.4 %collective-permute-start.12 = (bf16[64,1024]{1,0:T(8,128)(2,1)S(1)}, bf16[64,1024]{1,0:T(8,128)(2,1)S(1)}, u32[]{:S(2)}, u32[]{:S(2)}) collective-permute-start(bf16[64,1024]{1,0:T(8,128)(2,1)S(1)} %get-tuple-element.15.refs_0_), channel_id=1, source_target_pairs={{0,6},{1,7},{2,4},{3,5},{4,2},{5,3},{6,0},{7,1},{8,14},{9,15},{10,... | collective-permute-start | bytes 393224 | tf_op jit(solution)/shard_map/ppermute | solution.py:290
  18.5 7.7 %collective-permute-start.10 = (bf16[64,1024]{1,0:T(8,128)(2,1)S(1)}, bf16[64,1024]{1,0:T(8,128)(2,1)S(1)}, u32[]{:S(2)}, u32[]{:S(2)}) collective-permute-start(bf16[64,1024]{1,0:T(8,128)(2,1)S(1)} %get-tuple-element.15.refs_0_), channel_id=1, source_target_pairs={{0,4},{1,5},{2,6},{3,7},{4,0},{5,1},{6,2},{7,3},{8,12},{9,13},{10,... | collective-permute-start | bytes 393224 | tf_op jit(solution)/shard_map/ppermute | solution.py:290
  19.6 6.8 %collective-permute-start.8 = (bf16[64,1024]{1,0:T(8,128)(2,1)S(1)}, bf16[64,1024]{1,0:T(8,128)(2,1)S(1)}, u32[]{:S(2)}, u32[]{:S(2)}) collective-permute-start(bf16[64,1024]{1,0:T(8,128)(2,1)S(1)} %get-tuple-element.15.refs_0_), channel_id=1, source_target_pairs={{0,2},{1,3},{2,0},{3,1},{4,6},{5,7},{6,4},{7,5},{8,10},{9,11},{10,... | collective-permute-start | bytes 393224 | tf_op jit(solution)/shard_map/ppermute | solution.py:290
  20.5 10.2 %collective-permute-start.7 = (bf16[64,1024]{1,0:T(8,128)(2,1)S(1)}, bf16[64,1024]{1,0:T(8,128)(2,1)S(1)}, u32[]{:S(2)}, u32[]{:S(2)}) collective-permute-start(bf16[64,1024]{1,0:T(8,128)(2,1)S(1)} %get-tuple-element.15.refs_0_), channel_id=1, source_target_pairs={{0,1},{1,0},{2,3},{3,2},{4,5},{5,4},{6,7},{7,6},{8,9},{9,8},{10,11... | collective-permute-start | bytes 393224 | tf_op jit(solution)/shard_map/ppermute | solution.py:290
  24.3 6.5 %collective-permute-start.13 = (bf16[64,1024]{1,0:T(8,128)(2,1)S(1)}, bf16[64,1024]{1,0:T(8,128)(2,1)S(1)}, u32[]{:S(2)}, u32[]{:S(2)}) collective-permute-start(bf16[64,1024]{1,0:T(8,128)(2,1)S(1)} %collective-permute-done.12.refs_6_), channel_id=1, source_target_pairs={{0,1},{1,0},{2,3},{3,2},{4,5},{5,4},{6,7},{7,6},{8,9},{9,8},{10,11... | collective-permute-start | bytes 393224 | tf_op jit(solution)/shard_map/ppermute | solution.py:290
  26.3 4.5 %collective-permute-start.11 = (bf16[64,1024]{1,0:T(8,128)(2,1)S(1)}, bf16[64,1024]{1,0:T(8,128)(2,1)S(1)}, u32[]{:S(2)}, u32[]{:S(2)}) collective-permute-start(bf16[64,1024]{1,0:T(8,128)(2,1)S(1)} %collective-permute-done.10.refs_4_), channel_id=1, source_target_pairs={{0,1},{1,0},{2,3},{3,2},{4,5},{5,4},{6,7},{7,6},{8,9},{9,8},{10,11... | collective-permute-start | bytes 393224 | tf_op jit(solution)/shard_map/ppermute | solution.py:290
  26.4 4.4 %collective-permute-start.9 = (bf16[64,1024]{1,0:T(8,128)(2,1)S(1)}, bf16[64,1024]{1,0:T(8,128)(2,1)S(1)}, u32[]{:S(2)}, u32[]{:S(2)}) collective-permute-start(bf16[64,1024]{1,0:T(8,128)(2,1)S(1)} %collective-permute-done.8.refs_2_), channel_id=1, source_target_pairs={{0,1},{1,0},{2,3},{3,2},{4,5},{5,4},{6,7},{7,6},{8,9},{9,8},{10,11... | collective-permute-start | bytes 393224 | tf_op jit(solution)/shard_map/ppermute | solution.py:290
  36.3 24.8 %all-to-all-start = ((f32[32,4,128]{2,1,0:T(4,128)}), f32[32,4,128]{2,1,0:T(4,128)S(1)}, u32[]{:S(2)}, u32[]{:S(2)}) async-start(f32[32,4,128]{2,1,0:T(4,128)} %shard_map.63), calls=%async_computation | async-start | bytes 131072 | tf_op jit(solution)/shard_map/all_to_all | solution.py:351
  41.3 5.8 %collective-permute-start.14 = (bf16[144,256]{1,0:T(8,128)(2,1)S(1)}, bf16[144,256]{1,0:T(8,128)(2,1)S(1)}, u32[]{:S(2)}, u32[]{:S(2)}) collective-permute-start(bf16[144,256]{1,0:T(8,128)(2,1)S(1)} %get-tuple-element.19), channel_id=1, source_target_pairs={{0,8},{8,0},{16,24},{24,16},{1,9},{9,1},{17,25},{25,17},{2,10},{10... | collective-permute-start | bytes 221192 | tf_op jit(solution)/shard_map/ppermute | solution.py:290
  43.1 9.2 %collective-permute-start.15 = (bf16[144,256]{1,0:T(8,128)(2,1)S(1)}, bf16[144,256]{1,0:T(8,128)(2,1)S(1)}, u32[]{:S(2)}, u32[]{:S(2)}) collective-permute-start(bf16[144,256]{1,0:T(8,128)(2,1)S(1)} %get-tuple-element.20), channel_id=1, source_target_pairs={{0,16},{8,24},{16,0},{24,8},{1,17},{9,25},{17,1},{25,9},{2,18},{10... | collective-permute-start | bytes 221192 | tf_op jit(solution)/shard_map/ppermute | solution.py:290
  45.5 6.8 %collective-permute-start.16 = (bf16[144,256]{1,0:T(8,128)(2,1)S(1)}, bf16[144,256]{1,0:T(8,128)(2,1)S(1)}, u32[]{:S(2)}, u32[]{:S(2)}) collective-permute-start(bf16[144,256]{1,0:T(8,128)(2,1)S(1)} %get-tuple-element.21), channel_id=1, source_target_pairs={{0,24},{8,16},{16,8},{24,0},{1,25},{9,17},{17,9},{25,1},{2,26},{10... | collective-permute-start | bytes 221192 | tf_op jit(solution)/shard_map/ppermute | solution.py:290
  52.3 2.2 %copy-start.2 = (bf16[2048,1024]{1,0:T(8,128)(2,1)S(1)}, bf16[2048,1024]{1,0:T(8,128)(2,1)}, u32[]{:S(2)}) copy-start(bf16[2048,1024]{1,0:T(8,128)(2,1)} %refs_4_.1) | copy-start | bytes 12582916
  59.8 1.4 %copy-start.3 = (bf16[2048,512]{1,0:T(8,128)(2,1)}, bf16[2048,512]{1,0:T(8,128)(2,1)S(1)}, u32[]{:S(2)}) copy-start(bf16[2048,512]{1,0:T(8,128)(2,1)S(1)} %get-tuple-element.24.refs_3_) | copy-start | bytes 6291460
  61.1 1.6 %copy-start.4 = (bf16[2048,512]{1,0:T(8,128)(2,1)S(1)}, bf16[2048,512]{1,0:T(8,128)(2,1)}, u32[]{:S(2)}) copy-start(bf16[2048,512]{1,0:T(8,128)(2,1)} %copy-done.3) | copy-start | bytes 6291460

commit v2 on v1

v2 whole, which is shorter than its diff:
```python
import functools
import math

import jax
import jax.numpy as jnp
from jax import lax
from jax.experimental import pallas as pl
from jax.experimental.pallas import tpu as pltpu
from jax.sharding import PartitionSpec as P

perpendicular_weighting = 1.5
logit_divisor = 40.0
spill_offset = 2.0
BF = jnp.bfloat16
F32 = jnp.float32
I32 = jnp.int32
META = 8
VMEM_LIMIT = 24 * 1024 * 1024


def iota(shape, dim):
    return lax.broadcasted_iota(I32, shape, dim)


def nn(a, b):
    return lax.dot_general(a, b, (((1,), (0,)), ((), ())), preferred_element_type=F32)


def nt(a, b):
    return lax.dot_general(a, b, (((1,), (1,)), ((), ())), preferred_element_type=F32)


def as_bf(mask):
    return jnp.where(mask, 1.0, 0.0).astype(BF)


def call(kernel, outs, args, us=0.0, scratch=(), smem=0, hbm_in=(), hbm_out=(), vmem_in=(), vmem_out=()):
    specs = [pl.BlockSpec(memory_space=pltpu.SMEM)] * smem
    for i in range(smem, len(args)):
        specs.append(pl.BlockSpec(memory_space=pltpu.HBM if i in hbm_in else pltpu.VMEM))
    args = list(args)
    for i in hbm_in:
        args[i] = pltpu.with_memory_space_constraint(args[i], pltpu.HBM)
    for i in vmem_in:
        args[i] = pltpu.with_memory_space_constraint(args[i], pltpu.VMEM)
    return pl.pallas_call(
        kernel,
        out_shape=tuple(
            pltpu.VMEM(s, t) if i in vmem_out else jax.ShapeDtypeStruct(s, t)
            for i, (s, t) in enumerate(outs)
        ),
        in_specs=specs,
        out_specs=tuple(
            pl.BlockSpec(memory_space=pltpu.HBM if i in hbm_out else pltpu.VMEM)
            for i in range(len(outs))
        ),
        scratch_shapes=list(scratch),
        compiler_params=pltpu.CompilerParams(vmem_limit_bytes=VMEM_LIMIT),
        cost_estimate=pl.CostEstimate(
            flops=int(us * 5e8), bytes_accessed=int(us * 2e6), transcendentals=0
        ),
    )(*args)


def pack_kernel(me_ref, x_ref, prim_ref, sec_ref, out_ref, ids_ref, sems):
    rows = x_ref.shape[0]
    copies = [
        pltpu.make_async_copy(prim_ref, ids_ref.at[pl.ds(0, 1)], sems.at[0]),
        pltpu.make_async_copy(sec_ref, ids_ref.at[pl.ds(1, 1)], sems.at[1]),
        pltpu.make_async_copy(x_ref, out_ref.at[pl.ds(0, rows)], sems.at[2]),
    ]
    for copy in copies:
        copy.start()
    out_ref[rows:, 0:128] = jnp.zeros((META, 128), BF)
    for q in range(2):
        copies[q].wait()
        ids = ids_ref[q : q + 1, :]
        at = rows + 2 * q
        out_ref[at : at + 1, 0:rows] = (ids >> 8).astype(F32).astype(BF)
        out_ref[at + 1 : at + 2, 0:rows] = (ids & 255).astype(F32).astype(BF)
    copies[2].wait()


def tiles_in(src_ref, dst_ref, sems, tile, first=0):
    copies = []
    for i in range(dst_ref.shape[0] // tile):
        src = src_ref.at[pl.ds(first + i * tile, tile)]
        copies.append(pltpu.make_async_copy(src, dst_ref.at[pl.ds(i * tile, tile)], sems.at[i]))
    return copies


def load_kernel(tile, cent_ref, out_ref, token_ref, sems):
    copies = tiles_in(cent_ref, out_ref, sems, tile)
    for copy in copies:
        copy.start()
    token_ref[...] = jnp.zeros(token_ref.shape, F32)
    for copy in copies:
        copy.wait()


def rows_kernel(rows, cap, parts, shift, me_ref, *refs):
    blocks = refs[:parts]
    cent_ref, info_ref, out_ref = refs[parts:]
    group = rows * parts
    me = me_ref[0]
    spread = as_bf(iota((128, group), 0) == (iota((128, group), 1) % rows))
    lane_block = iota((META, group), 1) // rows
    bytes8 = jnp.zeros((META, group), F32)
    for s, ref in enumerate(blocks):
        got = nn(ref[rows : rows + META, 0:128], spread)
        bytes8 = bytes8 + jnp.where(lane_block == (me ^ s), got, 0.0)
    bytes8 = bytes8.astype(I32)
    prim = bytes8[0:1] * 256 + bytes8[1:2]
    sec = bytes8[2:3] * 256 + bytes8[3:4]
    before = (iota((group, group), 0) < iota((group, group), 1)) & (
        iota((group, group), 0) // rows == iota((group, group), 1) // rows
    )
    before = as_bf(before)
    ranks = []
    for ids in (prim, sec):
        same = iota((parts, group), 0) == (ids >> shift)
        count = nn(as_bf(same), before)
        ranks.append(jnp.sum(jnp.where(same, count, 0.0), axis=0, keepdims=True).astype(I32))
    base = (iota((1, group), 1) // rows) * cap
    slot_p = base + ranks[0]
    slot_s = base + ranks[1]
    info_ref[0:1, :] = prim
    info_ref[1:2, :] = sec
    info_ref[2:3, :] = slot_p
    info_ref[3:4, :] = slot_s
    info_ref[4:8, :] = jnp.zeros((4, group), I32)
    slots = cap * parts
    keep = (iota((slots, group), 0) == slot_p) & ((prim >> shift) == me)
    local = jnp.where(keep, (prim & ((1 << shift) - 1)) + 1, 0).astype(F32)
    row_id = jnp.sum(local, axis=1, keepdims=True).astype(I32) - 1
    pick = as_bf(iota((slots, 1 << shift), 1) == row_id)
    out_ref[...] = nn(pick, cent_ref[...]).astype(BF)


def slots_kernel(rows, cap, parts, dps, shift, me_ref, *refs):
    blocks = refs[:parts]
    info_ref, x_ref = refs[parts : parts + 2]
    outs = refs[parts + 2 : parts + 2 + dps]
    picked_ref = refs[-1]
    group = rows * parts
    slots = cap * parts
    me = me_ref[0]
    me_dp = me_ref[1]
    for s, ref in enumerate(blocks):
        at = pl.multiple_of((me ^ s) * rows, rows)
        x_ref[pl.ds(at, rows), :] = ref[0:rows, :]
    prim, sec = info_ref[0:1, :], info_ref[1:2, :]
    slot_p, slot_s = info_ref[2:3, :], info_ref[3:4, :]
    keep_p = (iota((slots, group), 0) == slot_p) & ((prim >> shift) == me)
    keep_s = (iota((slots, group), 0) == slot_s) & ((sec >> shift) == me)
    pick = jnp.concatenate([as_bf(keep_p), as_bf(keep_s)], axis=0)
    picked_ref[...] = nn(pick, x_ref[...]).astype(BF)
    where = iota((1, group), 1)
    meta = jnp.concatenate(
        [
            jnp.ones((1, group), F32),
            (where >> 8).astype(F32),
            (where & 255).astype(F32),
            jnp.zeros((5, group), F32),
        ],
        axis=0,
    ).astype(BF)
    mask = (1 << shift) - 1
    local_p, local_s = prim & mask, sec & mask
    loc = jnp.concatenate(
        [
            (local_p >> 8).astype(F32),
            (local_p & 255).astype(F32),
            (local_s >> 8).astype(F32),
            (local_s & 255).astype(F32),
            jnp.zeros((4, group), F32),
        ],
        axis=0,
    ).astype(BF)
    facts = jnp.concatenate([nt(meta, pick), nt(loc, pick)], axis=0).astype(BF)
    width = x_ref.shape[1] // dps
    for s in range(dps):
        at = pl.multiple_of((me_dp ^ s) * width, width)
        outs[s][0 : 2 * slots, :] = picked_ref[:, pl.ds(at, width)]
        outs[s][2 * slots :, 0:128] = facts


def base_kernel(tile, x_ref, cent_ref, out_ref, token_ref):
    x = x_ref[...]
    for k in range(0, cent_ref.shape[0], tile):
        c = cent_ref[k : k + tile, :]
        cf = c.astype(F32)
        out_ref[k : k + tile, :] = 2.0 * nt(c, x) - jnp.sum(cf * cf, axis=1, keepdims=True)
    token_ref[...] = jnp.zeros(token_ref.shape, F32)


def score_kernel(rows, cap, parts, shift, tile, me_ref, *refs):
    owned = refs[:parts]
    x_ref, info_ref, cent_ref, base_ref, out_ref, r_ref, t_ref = refs[parts:]
    group = rows * parts
    slots = cap * parts
    me = me_ref[0]
    dim = x_ref.shape[1]
    prim, sec, slot_p = info_ref[0:1, :], info_ref[1:2, :], info_ref[2:3, :]
    place = ((prim >> shift) ^ me) * slots + slot_p
    place = jnp.transpose(jnp.broadcast_to(place.astype(F32), (128, group)))[:, 0:1].astype(I32)
    pick = as_bf(iota((group, parts * slots), 1) == place)
    found = nn(pick, jnp.concatenate([ref[...] for ref in owned], axis=0))
    x = x_ref[...]
    r_ref[...] = (x.astype(F32) - found).astype(BF)
    r = r_ref[...]
    diag = iota((group, group), 0) == iota((group, group), 1)
    rx = jnp.sum(jnp.where(diag, nt(x, r), 0.0), axis=0, keepdims=True)
    rr = jnp.sum(jnp.where(diag, nt(r, r), 0.0), axis=0, keepdims=True)
    spread = rr * (1.0 / dim) + 1e-05
    gain = perpendicular_weighting / (dim * spread)
    sec_row = jnp.where((sec >> shift) == me, sec & ((1 << shift) - 1), -1)

    top = jnp.full((1, group), -jnp.inf, F32)
    picked = jnp.zeros((1, group), F32)
    count = cent_ref.shape[0] // tile
    for i in range(count):
        at = slice(i * tile, (i + 1) * tile)
        gap = rx - nt(cent_ref[at, :], r)
        t = (base_ref[at, :] - gain * (gap * gap)) * (1.0 / logit_divisor)
        t_ref[at, :] = t
        hit = (iota((tile, group), 0) + i * tile) == sec_row
        picked = picked + jnp.sum(jnp.where(hit, t, 0.0), axis=0, keepdims=True)
        top = jnp.maximum(top, jnp.max(t, axis=0, keepdims=True))

    total = jnp.zeros((1, group), F32)
    for i in range(count):
        e = jnp.exp(t_ref[i * tile : (i + 1) * tile, :] - top)
        total = total + jnp.sum(e, axis=0, keepdims=True)
    part = top + jnp.log(total)
    lines = [part[:, i : i + 128] for i in range(0, group, 128)]
    lines += [picked[:, i : i + 128] for i in range(0, group, 128)]
    packed = jnp.concatenate(lines, axis=0)
    out_ref[...] = jnp.broadcast_to(packed[None], out_ref.shape)


def split(a):
    high = a.astype(BF)
    return high, (a - high.astype(F32)).astype(BF)


def lists_kernel(cap, parts, dps, shift, group, tile, me_ref, *refs):
    blocks = refs[:dps]
    cent_ref, sum_ref, diff_ref, ids_ref, lane_ref, c_ref, blocks_ref, sems = refs[dps:]
    slots = cap * parts
    cents = 1 << shift
    width = blocks[0].shape[1]
    at = pl.multiple_of(me_ref[1] * width, width)
    copies = [pltpu.make_async_copy(cent_ref.at[:, pl.ds(at, width)], c_ref, sems.at[0])]
    for s in range(1, dps):
        copies.append(pltpu.make_async_copy(blocks[s], blocks_ref.at[s - 1], sems.at[s]))
    for copy in copies:
        copy.start()
    for copy in copies:
        copy.wait()
    diffs, ids_p, ids_s = [], [], []
    for s in range(dps):
        ref = blocks_ref.at[s - 1] if s else blocks[0]
        facts = ref[2 * slots :, 0:128].astype(F32)
        valid = facts[0:1, :] > 0.0
        second = iota((1, 128), 1) >= slots
        high = jnp.where(second, facts[10:11, :], facts[8:9, :])
        low = jnp.where(second, facts[11:12, :], facts[9:10, :])
        ids = jnp.where(valid, high * 256.0 + low, -1.0)
        where = jnp.where(valid, facts[1:2, :] * 256.0 + facts[2:3, :], -1.0)
        ids_p.append(ids[:, 0:slots])
        ids_s.append(ids[:, slots : 2 * slots])
        ids_col = jnp.transpose(jnp.broadcast_to(ids, (128, 128)))[:, 0:1].astype(I32)
        where_col = jnp.transpose(jnp.broadcast_to(where, (128, 128)))[slots:, 0:1].astype(I32)
        lane_ref[s * slots : (s + 1) * slots, :] = as_bf(
            iota((slots, group), 1) == where_col
        )
        pick = as_bf(iota((128, cents), 1) == ids_col)
        rows = nn(pick, c_ref[...])
        diff = ref[0 : 2 * slots, :].astype(F32) - rows
        diff_ref[s * slots : (s + 1) * slots, :] = diff[slots:, :]
        diffs.append(diff[0:slots, :])
    high, low = split(jnp.concatenate(diffs, axis=0))
    ids_p = jnp.concatenate(ids_p, axis=1).astype(I32)
    ids_s = jnp.concatenate(ids_s, axis=1).astype(I32)
    ids_ref[...] = jnp.broadcast_to(ids_s, ids_ref.shape)

    @pl.loop(0, cents, step=tile)
    def _(k):
        k = pl.multiple_of(k, tile)
        hot = as_bf((iota((tile, dps * slots), 0) + k) == ids_p)
        sum_ref[pl.ds(k, tile), :] = nn(hot, high) + nn(hot, low)


def final_kernel(rows, cap, parts, dps, group, tile, log_count, me_ref, *refs):
    got_ref, sum_ref, diff_ref, ids_ref, lane_ref, cost_ref, out_ref, weight_ref, part_ref, sems = refs
    slots = cap * parts
    lines = group // 128
    me = me_ref[0]
    part = got_ref[:, 0:lines, :].reshape(dps, parts, lines, 128)
    top = jnp.max(part, axis=1)
    lse = top + jnp.log(jnp.sum(jnp.exp(part - top[:, None]), axis=1))
    picked = jnp.concatenate(
        [got_ref[pl.ds(d * parts + me, 1), lines : 2 * lines, :] for d in range(dps)], axis=0
    )
    z = picked - lse + log_count + spill_offset
    e = jnp.exp(-jnp.abs(z))
    weight = jnp.where(z >= 0.0, 1.0, e) / (1.0 + e)
    for d in range(dps):
        for i in range(lines):
            at = slice(i * 128, (i + 1) * 128)
            weight_ref[d : d + 1, at] = weight[d, i : i + 1, :]
            weight_ref[dps + d : dps + d + 1, at] = lse[d, i : i + 1, :]
    terms = []
    for s in range(dps):
        at = slice(s * slots, (s + 1) * slots)
        mine = weight_ref[pl.ds(me_ref[1] ^ s, 1), :]
        column = jnp.sum(lane_ref[at, :].astype(F32) * mine, axis=1, keepdims=True)
        terms.append(column * diff_ref[at, :])
    high, low = split(jnp.concatenate(terms, axis=0))
    ids = ids_ref[0:1, :]
    count = out_ref.shape[0] // tile
    copies = []
    for i in range(count):
        at = pl.ds(i * tile, tile)
        hot = as_bf((iota((tile, dps * slots), 0) + i * tile) == ids)
        part_ref[at, :] = (sum_ref[at, :] + (nn(hot, high) + nn(hot, low))).astype(BF)
        copies.append(pltpu.make_async_copy(part_ref.at[at], out_ref.at[at], sems.at[i]))
        copies[i].start()
    flat = weight_ref[pl.ds(dps + me_ref[1], 1), :]
    cost = jnp.zeros((1, rows), F32)
    for b in range(parts):
        cost = cost + jnp.where(me == b, flat[:, b * rows : (b + 1) * rows], 0.0)
    cost_ref[...] = cost - log_count
    for copy in copies:
        copy.wait()


def swap(a, axis, count, step):
    return lax.ppermute(a, axis, [(i, i ^ step) for i in range(count)])


def after(a, token):
    return lax.optimization_barrier((a, token))[0]


def far_blocks(a, count):
    return [a] + [swap(a, "cent", count, s) for s in range(2, count, 2)]


def all_blocks(far, token, count):
    near = [swap(far[0], "cent", count, 1)]
    near += [swap(after(a, token), "cent", count, 1) for a in far[1:]]
    return [a for pair in zip(far, near) for a in pair]


def per_device(vectors, centroids, primary, secondary):
    rows, dim = vectors.shape
    cents = centroids.shape[0]
    parts = lax.axis_size("cent")
    dps = lax.axis_size("dp")
    group = rows * parts
    cap = 2 * rows // parts
    slots = cap * parts
    shift = cents.bit_length() - 1
    assert cents == 1 << shift and 2 * slots == 128
    width = dim // dps
    tile = 256
    lines = group // 128
    token_out = ((8, 128), F32)
    me = jnp.stack([lax.axis_index("cent"), lax.axis_index("dp")]).astype(I32)

    (packed,) = call(
        pack_kernel,
        [((rows + META, dim), BF)],
        [me, vectors, primary.reshape(1, rows), secondary.reshape(1, rows)],
        smem=1,
        hbm_in=(1, 2, 3),
        scratch=[pltpu.VMEM((2, rows), I32), pltpu.SemaphoreType.DMA((3,))],
    )
    packed, cent = lax.optimization_barrier((packed, centroids))
    far = far_blocks(packed, parts)
    cent, token = call(
        functools.partial(load_kernel, tile),
        [((cents, dim), BF), token_out],
        [cent],
        us=3.0,
        hbm_in=(0,),
        vmem_out=(0,),
        scratch=[pltpu.SemaphoreType.DMA((cents // tile,))],
    )
    blocks = all_blocks(far, token, parts)
    info, owned = call(
        functools.partial(rows_kernel, rows, cap, parts, shift),
        [((8, group), I32), ((slots, dim), BF)],
        [me, *blocks, cent],
        us=2.0,
        smem=1,
        vmem_in=(parts + 1,),
    )
    far = far_blocks(owned, parts)
    x_all, *columns = call(
        functools.partial(slots_kernel, rows, cap, parts, dps, shift),
        [((group, dim), BF)] + [((2 * slots + 16, width), BF)] * dps,
        [me, *blocks, info],
        us=1.0,
        smem=1,
        scratch=[pltpu.VMEM((2 * slots, dim), BF)],
    )
    columns = [columns[0]] + [swap(columns[s], "dp", dps, s) for s in range(1, dps)]
    base, token = call(
        functools.partial(base_kernel, tile),
        [((cents, group), F32), token_out],
        [x_all, cent],
        us=2.0,
        vmem_in=(1,),
    )
    owned = all_blocks(far, token, parts)
    (sent,) = call(
        functools.partial(score_kernel, rows, cap, parts, shift, tile),
        [((dps * parts, 2 * lines, 128), F32)],
        [me, *owned, x_all, info, cent, base],
        us=6.0,
        smem=1,
        vmem_in=(parts + 3,),
        scratch=[pltpu.VMEM((group, dim), BF), pltpu.VMEM((cents, group), F32)],
    )
    sent, columns[0] = lax.optimization_barrier((sent, columns[0]))
    got = lax.all_to_all(sent, ("dp", "cent"), 0, 0, tiled=True)
    list_sum, diff, ids, lane = call(
        functools.partial(lists_kernel, cap, parts, dps, shift, group, tile),
        [
            ((cents, width), F32),
            ((dps * slots, width), F32),
            ((8, dps * slots), I32),
            ((dps * slots, group), BF),
        ],
        [me, *columns, centroids],
        smem=1,
        hbm_in=tuple(range(2, dps + 2)),
        us=4.0,
        scratch=[
            pltpu.VMEM((cents, width), BF),
            pltpu.VMEM((dps - 1, 2 * slots + 16, width), BF),
            pltpu.SemaphoreType.DMA((dps,)),
        ],
    )
    log_count = math.log(cents * parts)
    cost, out = call(
        functools.partial(final_kernel, rows, cap, parts, dps, group, tile, log_count),
        [((1, rows), F32), ((cents, width), BF)],
        [me, got, list_sum, diff, ids, lane],
        smem=1,
        hbm_out=(1,),
        scratch=[
            pltpu.VMEM((2 * dps, group), F32),
            pltpu.VMEM((cents, width), BF),
            pltpu.SemaphoreType.DMA((cents // tile,)),
        ],
    )
    return cost.reshape(rows), out


def solution(mesh):
    in_specs = (P(("dp", "cent"), None), P("cent", None), P(("dp", "cent")), P(("dp", "cent")))
    out_specs = (P(("dp", "cent")), P("cent", "dp"))
    return jax.shard_map(
        per_device, mesh=mesh, in_specs=in_specs, out_specs=out_specs, check_vma=False
    )
```

time: 67.8 us -> 48.3 us (0.71)
  waiting for transfers between devices: 17.9 us -> 7.32 us
  local copies, waits for them, and re-layouts: 9.46 us -> 1.26 us
  Pallas kernels: 21.2 us -> 20 us
  starting transfers between devices: 18 us -> 18.7 us
    ppermute x17, waiting for transfers between devices: 17.9 us -> 5.8 us  [swap(): return lax.ppermute(a, axis, [(i, i ^ step) for i in range(count)])]
    unnamed x16 -> x6, local copies, waits for them, and re-layouts: 9.46 us -> 1.26 us
    all_to_all x1, waiting for transfers between devices: 0.01 us -> 1.51 us  [per_device(): got = lax.all_to_all(sent, ('dp', 'cent'), 0, 0, tiled=True)]
    pallas_call x7 -> x8, Pallas kernels: 21.2 us -> 20 us  [call(): pl.pallas_call(kernel, out_shape=tuple((pltpu.VMEM(s, t) if i in vmem_out...]
  transfers between devices with their start and end apart: 18 -> 18, of which waited for: 10 -> 9; matrix products, arithmetic and copies ran while one was open for 0% -> 0% of each run, Pallas kernels for 14% -> 29%
where the time goes in v2:
time: 48.3 us; the launch traced here: 48.1 us
  Pallas kernels  20 us (41%)
  starting transfers between devices  18.7 us (39%)
  waiting for transfers between devices  7.32 us (15%)
  local copies, waits for them, and re-layouts  1.26 us (3%)
  between operations  0.74 us (2%)
    pallas_call x8, Pallas kernels, call(): pl.pallas_call(kernel, out_shape=tuple((pltpu.VMEM(s, t) if i in vmem_out...  20 us
    ppermute x17, starting transfers between devices, swap(): return lax.ppermute(a, axis, [(i, i ^ step) for i in range(count)])  13.6 us
    ppermute x17, waiting for transfers between devices, swap(): return lax.ppermute(a, axis, [(i, i ^ step) for i in range(count)])  5.8 us
    all_to_all x1, starting transfers between devices, per_device(): got = lax.all_to_all(sent, ('dp', 'cent'), 0, 0, tiled=True)  5.01 us
    all_to_all x1, waiting for transfers between devices, per_device(): got = lax.all_to_all(sent, ('dp', 'cent'), 0, 0, tiled=True)  1.51 us
    unnamed x6, local copies, waits for them, and re-layouts  1.26 us
  transfers between devices with their start and end apart: 18, of which 9 were waited for; matrix products, arithmetic and copies ran while one was open for 0% of the time, Pallas kernels for 29%

profile of v2, /device:TPU:0, one launch (start us, length us, event | category | flops | bytes accessed | tf_op | source)
XLA Modules:
  0.0 48.1 jit_solution(18126780625952075729)
XLA Ops:
  0.6 0.1 pad_add_fusion.me_ref
  0.7 1.4 %shard_map.59.refs_0_ = bf16[40,1024]{1,0:T(8,128)(2,1)S(1)} custom-call(s32[2]{0:T(128)S(1)} %pad_add_fusion.me_ref, bf16[32,1024]{1,0:T(8,128)(2,1)} %x_ref.1, s32[1,32]{1,0:T(1,128)} %bitcast.5, s32[1,32]{1,0:T(1,128)} %bitcast.6), custom_call_target="tpu_custom_call" | custom-call | tf_op jit(solution)/shard_map/pallas_call | solution.py:46
  2.2 4.0 %collective-permute-start.5 = (bf16[40,1024]{1,0:T(8,128)(2,1)S(1)}, bf16[40,1024]{1,0:T(8,128)(2,1)S(1)}, u32[]{:S(2)}, u32[]{:S(2)}) collective-permute-start(bf16[40,1024]{1,0:T(8,128)(2,1)S(1)} %shard_map.59.refs_0_), channel_id=1, source_target_pairs={{0,6},{1,7},{2,4},{3,5},{4,2},{5,3},{6,0},{7,1},{8,14},{9,15},{10,... | collective-permute-start | bytes 245768 | tf_op jit(solution)/shard_map/ppermute | solution.py:340
  6.1 0.5 %collective-permute-start.3 = (bf16[40,1024]{1,0:T(8,128)(2,1)S(1)}, bf16[40,1024]{1,0:T(8,128)(2,1)S(1)}, u32[]{:S(2)}, u32[]{:S(2)}) collective-permute-start(bf16[40,1024]{1,0:T(8,128)(2,1)S(1)} %shard_map.59.refs_0_), channel_id=1, source_target_pairs={{0,4},{1,5},{2,6},{3,7},{4,0},{5,1},{6,2},{7,3},{8,12},{9,13},{10,... | collective-permute-start | bytes 245768 | tf_op jit(solution)/shard_map/ppermute | solution.py:340
  6.6 0.1 collective-permute-start.1
  6.8 0.0 collective-permute-start
  6.8 2.8 %shard_map.60 = (bf16[2048,1024]{1,0:T(8,128)(2,1)S(1)}, f32[8,128]{1,0:T(8,128)}) custom-call(bf16[2048,1024]{1,0:T(8,128)(2,1)} %refs_4_.1), custom_call_target="tpu_custom_call" | custom-call | flops 1500000000 | bytes 6000000 | tf_op jit(solution)/shard_map/pallas_call | solution.py:46
  9.6 0.0 collective-permute-done.5.refs_6_
  9.6 1.0 %collective-permute-done.3.refs_4_ = bf16[40,1024]{1,0:T(8,128)(2,1)S(1)} collective-permute-done((bf16[40,1024]{1,0:T(8,128)(2,1)S(1)}, bf16[40,1024]{1,0:T(8,128)(2,1)S(1)}, u32[]{:S(2)}, u32[]{:S(2)}) %collective-permute-start.3) | collective-permute-done | bytes 81952 | tf_op jit(solution)/shard_map/ppermute | solution.py:340
  10.6 0.5 %collective-permute-done.1.refs_2_ = bf16[40,1024]{1,0:T(8,128)(2,1)S(1)} collective-permute-done((bf16[40,1024]{1,0:T(8,128)(2,1)S(1)}, bf16[40,1024]{1,0:T(8,128)(2,1)S(1)}, u32[]{:S(2)}, u32[]{:S(2)}) %collective-permute-start.1) | collective-permute-done | bytes 81952 | tf_op jit(solution)/shard_map/ppermute | solution.py:340
  11.1 0.0 collective-permute-start.2
  11.1 0.5 %collective-permute-start.4 = (bf16[40,1024]{1,0:T(8,128)(2,1)S(1)}, bf16[40,1024]{1,0:T(8,128)(2,1)S(1)}, u32[]{:S(2)}, u32[]{:S(2)}) collective-permute-start(bf16[40,1024]{1,0:T(8,128)(2,1)S(1)} %collective-permute-done.3.refs_4_), channel_id=1, source_target_pairs={{0,1},{1,0},{2,3},{3,2},{4,5},{5,4},{6,7},{7,6},{8,9},{9,8},{10,11... | collective-permute-start | bytes 245768 | tf_op jit(solution)/shard_map/ppermute | solution.py:340
  11.6 0.0 collective-permute-start.6
  11.6 0.0 collective-permute-done.refs_1_
  11.6 0.8 %collective-permute-done.2.refs_3_ = bf16[40,1024]{1,0:T(8,128)(2,1)S(1)} collective-permute-done((bf16[40,1024]{1,0:T(8,128)(2,1)S(1)}, bf16[40,1024]{1,0:T(8,128)(2,1)S(1)}, u32[]{:S(2)}, u32[]{:S(2)}) %collective-permute-start.2) | collective-permute-done | bytes 81952 | tf_op jit(solution)/shard_map/ppermute | solution.py:340
  12.4 0.2 collective-permute-done.4.refs_5_
  12.5 0.4 collective-permute-done.6.refs_7_
  12.9 1.7 %shard_map.61 = (s32[8,256]{1,0:T(8,128)S(1)}, bf16[64,1024]{1,0:T(8,128)(2,1)S(1)}) custom-call(s32[2]{0:T(128)S(1)} %pad_add_fusion.me_ref, bf16[40,1024]{1,0:T(8,128)(2,1)S(1)} %shard_map.59.refs_0_, bf16[40,1024]{1,0:T(8,128)(2,1)S(1)} %collective-permute-done.refs_1_, bf16[40,1024]{1,0:T(8,128)(2,1)S(1)} %collective-permute-done.1.refs_2_, ...), custom_call_target="tpu_custom_call" | custom-call | flops 1000000000 | bytes 4000000 | tf_op jit(solution)/shard_map/pallas_call | solution.py:46
  14.6 1.7 %collective-permute-start.12 = (bf16[64,1024]{1,0:T(8,128)(2,1)S(1)}, bf16[64,1024]{1,0:T(8,128)(2,1)S(1)}, u32[]{:S(2)}, u32[]{:S(2)}) collective-permute-start(bf16[64,1024]{1,0:T(8,128)(2,1)S(1)} %get-tuple-element.36.refs_0_), channel_id=1, source_target_pairs={{0,6},{1,7},{2,4},{3,5},{4,2},{5,3},{6,0},{7,1},{8,14},{9,15},{10,... | collective-permute-start | bytes 393224 | tf_op jit(solution)/shard_map/ppermute | solution.py:340
  16.3 0.8 %collective-permute-start.10 = (bf16[64,1024]{1,0:T(8,128)(2,1)S(1)}, bf16[64,1024]{1,0:T(8,128)(2,1)S(1)}, u32[]{:S(2)}, u32[]{:S(2)}) collective-permute-start(bf16[64,1024]{1,0:T(8,128)(2,1)S(1)} %get-tuple-element.36.refs_0_), channel_id=1, source_target_pairs={{0,4},{1,5},{2,6},{3,7},{4,0},{5,1},{6,2},{7,3},{8,12},{9,13},{10,... | collective-permute-start | bytes 393224 | tf_op jit(solution)/shard_map/ppermute | solution.py:340
  17.1 1.0 %collective-permute-start.8 = (bf16[64,1024]{1,0:T(8,128)(2,1)S(1)}, bf16[64,1024]{1,0:T(8,128)(2,1)S(1)}, u32[]{:S(2)}, u32[]{:S(2)}) collective-permute-start(bf16[64,1024]{1,0:T(8,128)(2,1)S(1)} %get-tuple-element.36.refs_0_), channel_id=1, source_target_pairs={{0,2},{1,3},{2,0},{3,1},{4,6},{5,7},{6,4},{7,5},{8,10},{9,11},{10,... | collective-permute-start | bytes 393224 | tf_op jit(solution)/shard_map/ppermute | solution.py:340
  18.2 0.0 collective-permute-start.7
  18.2 0.9 %shard_map.62 = (bf16[256,1024]{1,0:T(8,128)(2,1)S(1)}, bf16[144,256]{1,0:T(8,128)(2,1)S(1)}, bf16[144,256]{1,0:T(8,128)(2,1)S(1)}, bf16[144,256]{1,0:T(8,128)(2,1)S(1)}, bf16[144,256]{1,0:T(8,128)(2,1)S(1)}) custom-call(s32[2]{0:T(128)S(1)} %pad_add_fusion.me_ref, bf16[40,1024]{1,0:T(8,128)(2,1)S(1)} %shard_map.59.refs_0_, ...), custom_call_target="tpu_custom_call" | custom-call | flops 500000000 | bytes 2000000 | tf_op jit(solution)/shard_map/pallas_call | solution.py:46
  19.0 2.0 %shard_map.63 = (f32[2048,256]{1,0:T(8,128)S(1)}, f32[8,128]{1,0:T(8,128)}) custom-call(bf16[256,1024]{1,0:T(8,128)(2,1)S(1)} %get-tuple-element.38.x_ref.refs_8_, bf16[2048,1024]{1,0:T(8,128)(2,1)S(1)} %get-tuple-element.35.refs_8_.cent_ref.refs_10_), custom_call_target="tpu_custom_call" | custom-call | flops 1000000000 | bytes 4000000 | tf_op jit(solution)/shard_map/pallas_call | solution.py:46
  21.0 0.9 %collective-permute-done.12.refs_6_ = bf16[64,1024]{1,0:T(8,128)(2,1)S(1)} collective-permute-done((bf16[64,1024]{1,0:T(8,128)(2,1)S(1)}, bf16[64,1024]{1,0:T(8,128)(2,1)S(1)}, u32[]{:S(2)}, u32[]{:S(2)}) %collective-permute-start.12) | collective-permute-done | bytes 131104 | tf_op jit(solution)/shard_map/ppermute | solution.py:340
  22.0 2.0 %collective-permute-done.10.refs_4_ = bf16[64,1024]{1,0:T(8,128)(2,1)S(1)} collective-permute-done((bf16[64,1024]{1,0:T(8,128)(2,1)S(1)}, bf16[64,1024]{1,0:T(8,128)(2,1)S(1)}, u32[]{:S(2)}, u32[]{:S(2)}) %collective-permute-start.10) | collective-permute-done | bytes 131104 | tf_op jit(solution)/shard_map/ppermute | solution.py:340
  23.9 0.1 collective-permute-done.8.refs_2_
  24.1 0.0 collective-permute-start.9
  24.1 0.5 %collective-permute-start.11 = (bf16[64,1024]{1,0:T(8,128)(2,1)S(1)}, bf16[64,1024]{1,0:T(8,128)(2,1)S(1)}, u32[]{:S(2)}, u32[]{:S(2)}) collective-permute-start(bf16[64,1024]{1,0:T(8,128)(2,1)S(1)} %collective-permute-done.10.refs_4_), channel_id=1, source_target_pairs={{0,1},{1,0},{2,3},{3,2},{4,5},{5,4},{6,7},{7,6},{8,9},{9,8},{10,11... | collective-permute-start | bytes 393224 | tf_op jit(solution)/shard_map/ppermute | solution.py:340
  24.6 0.0 collective-permute-start.13
  24.6 1.6 %collective-permute-start.14 = (bf16[144,256]{1,0:T(8,128)(2,1)S(1)}, bf16[144,256]{1,0:T(8,128)(2,1)S(1)}, u32[]{:S(2)}, u32[]{:S(2)}) collective-permute-start(bf16[144,256]{1,0:T(8,128)(2,1)S(1)} %get-tuple-element.47), channel_id=1, source_target_pairs={{0,8},{8,0},{16,24},{24,16},{1,9},{9,1},{17,25},{25,17},{2,10},{10... | collective-permute-start | bytes 221192 | tf_op jit(solution)/shard_map/ppermute | solution.py:340
  26.1 0.0 collective-permute-done.7.refs_1_
  26.1 2.6 %collective-permute-start.15 = (bf16[144,256]{1,0:T(8,128)(2,1)S(1)}, bf16[144,256]{1,0:T(8,128)(2,1)S(1)}, u32[]{:S(2)}, u32[]{:S(2)}) collective-permute-start(bf16[144,256]{1,0:T(8,128)(2,1)S(1)} %get-tuple-element.48), channel_id=1, source_target_pairs={{0,16},{8,24},{16,0},{24,8},{1,17},{9,25},{17,1},{25,9},{2,18},{10... | collective-permute-start | bytes 221192 | tf_op jit(solution)/shard_map/ppermute | solution.py:340
  28.7 0.0 collective-permute-done.9.refs_3_
  28.7 0.3 collective-permute-start.16
  29.0 0.0 collective-permute-done.11.refs_5_
  29.0 0.0 collective-permute-done.13.refs_7_
  29.0 4.0 %shard_map.64 = f32[32,4,128]{2,1,0:T(4,128)} custom-call(s32[2]{0:T(128)S(1)} %pad_add_fusion.me_ref, bf16[64,1024]{1,0:T(8,128)(2,1)S(1)} %get-tuple-element.36.refs_0_, bf16[64,1024]{1,0:T(8,128)(2,1)S(1)} %collective-permute-done.7.refs_1_, bf16[64,1024]{1,0:T(8,128)(2,1)S(1)} %collective-permute-done.8.refs_2_, ...), custom_call_target="tpu_custom_call" | custom-call | flops 3000000000 | bytes 12000000 | tf_op jit(solution)/shard_map/pallas_call | solution.py:46
  33.0 5.0 %all-to-all-start = ((f32[32,4,128]{2,1,0:T(4,128)}), f32[32,4,128]{2,1,0:T(4,128)S(1)}, u32[]{:S(2)}, u32[]{:S(2)}) async-start(f32[32,4,128]{2,1,0:T(4,128)} %shard_map.64), calls=%async_computation | async-start | bytes 131072 | tf_op jit(solution)/shard_map/all_to_all | solution.py:429
  38.0 0.0 collective-permute-done.14.refs_1_
  38.0 0.0 copy-start
  38.0 0.0 collective-permute-done.15.refs_2_
  38.0 0.0 copy-start.1
  38.0 0.0 collective-permute-done.16.refs_3_
  38.0 0.6 %copy-done = bf16[144,256]{1,0:T(8,128)(2,1)} copy-done((bf16[144,256]{1,0:T(8,128)(2,1)}, bf16[144,256]{1,0:T(8,128)(2,1)S(1)}, u32[]{:S(2)}) %copy-start) | copy-done | bytes 73752
  38.6 0.0 copy-done.1
  38.7 0.0 copy-start.2
  38.7 0.6 %copy-done.2 = bf16[144,256]{1,0:T(8,128)(2,1)} copy-done((bf16[144,256]{1,0:T(8,128)(2,1)}, bf16[144,256]{1,0:T(8,128)(2,1)S(1)}, u32[]{:S(2)}) %copy-start.2) | copy-done | bytes 73752
  39.3 4.6 %shard_map.65 = (f32[2048,256]{1,0:T(8,128)S(1)}, f32[256,256]{1,0:T(8,128)S(1)}, s32[8,256]{1,0:T(8,128)S(1)}, bf16[256,256]{1,0:T(8,128)(2,1)S(1)}) custom-call(s32[2]{0:T(128)S(1)} %pad_add_fusion.me_ref, bf16[144,256]{1,0:T(8,128)(2,1)S(1)} %get-tuple-element.46.refs_0_, bf16[144,256]{1,0:T(8,128)(2,1)} %copy-done, bf16[144,256]{1,0:T(8,128)(2,1)} %copy-done.1, ...), custom_call_target="tpu_custom_call" | custom-call | flops 2000000000 | bytes 8000000 | tf_op jit(solution)/shard_map/pallas_call | solution.py:46
  43.9 1.5 %all-to-all-done.refs_0_ = f32[32,4,128]{2,1,0:T(4,128)S(1)} async-done(((f32[32,4,128]{2,1,0:T(4,128)}), f32[32,4,128]{2,1,0:T(4,128)S(1)}, u32[]{:S(2)}, u32[]{:S(2)}) %all-to-all-start) | async-done | bytes 65568 | tf_op jit(solution)/shard_map/all_to_all | solution.py:429
  45.4 2.7 %shard_map.66 = (f32[1,32]{1,0:T(1,128)}, bf16[2048,256]{1,0:T(8,128)(2,1)}) custom-call(s32[2]{0:T(128)S(1)} %pad_add_fusion.me_ref, f32[32,4,128]{2,1,0:T(4,128)S(1)} %all-to-all-done.refs_0_, f32[2048,256]{1,0:T(8,128)S(1)} %get-tuple-element.50.refs_1_, f32[256,256]{1,0:T(8,128)S(1)} %get-tuple-element.51.refs_2_, ...), custom_call_target="tpu_custom_call" | custom-call | tf_op jit(solution)/shard_map/pallas_call | solution.py:46
Async XLA Ops:
  2.2 7.5 %collective-permute-start.5 = (bf16[40,1024]{1,0:T(8,128)(2,1)S(1)}, bf16[40,1024]{1,0:T(8,128)(2,1)S(1)}, u32[]{:S(2)}, u32[]{:S(2)}) collective-permute-start(bf16[40,1024]{1,0:T(8,128)(2,1)S(1)} %shard_map.59.refs_0_), channel_id=1, source_target_pairs={{0,6},{1,7},{2,4},{3,5},{4,2},{5,3},{6,0},{7,1},{8,14},{9,15},{10,... | collective-permute-start | bytes 245768 | tf_op jit(solution)/shard_map/ppermute | solution.py:340
  6.1 4.4 %collective-permute-start.3 = (bf16[40,1024]{1,0:T(8,128)(2,1)S(1)}, bf16[40,1024]{1,0:T(8,128)(2,1)S(1)}, u32[]{:S(2)}, u32[]{:S(2)}) collective-permute-start(bf16[40,1024]{1,0:T(8,128)(2,1)S(1)} %shard_map.59.refs_0_), channel_id=1, source_target_pairs={{0,4},{1,5},{2,6},{3,7},{4,0},{5,1},{6,2},{7,3},{8,12},{9,13},{10,... | collective-permute-start | bytes 245768 | tf_op jit(solution)/shard_map/ppermute | solution.py:340
  6.6 4.4 %collective-permute-start.1 = (bf16[40,1024]{1,0:T(8,128)(2,1)S(1)}, bf16[40,1024]{1,0:T(8,128)(2,1)S(1)}, u32[]{:S(2)}, u32[]{:S(2)}) collective-permute-start(bf16[40,1024]{1,0:T(8,128)(2,1)S(1)} %shard_map.59.refs_0_), channel_id=1, source_target_pairs={{0,2},{1,3},{2,0},{3,1},{4,6},{5,7},{6,4},{7,5},{8,10},{9,11},{10,... | collective-permute-start | bytes 245768 | tf_op jit(solution)/shard_map/ppermute | solution.py:340
  6.8 4.8 %collective-permute-start = (bf16[40,1024]{1,0:T(8,128)(2,1)S(1)}, bf16[40,1024]{1,0:T(8,128)(2,1)S(1)}, u32[]{:S(2)}, u32[]{:S(2)}) collective-permute-start(bf16[40,1024]{1,0:T(8,128)(2,1)S(1)} %shard_map.59.refs_0_), channel_id=1, source_target_pairs={{0,1},{1,0},{2,3},{3,2},{4,5},{5,4},{6,7},{7,6},{8,9},{9,8},{10,11... | collective-permute-start | bytes 245768 | tf_op jit(solution)/shard_map/ppermute | solution.py:340
  11.1 1.3 %collective-permute-start.2 = (bf16[40,1024]{1,0:T(8,128)(2,1)S(1)}, bf16[40,1024]{1,0:T(8,128)(2,1)S(1)}, u32[]{:S(2)}, u32[]{:S(2)}) collective-permute-start(bf16[40,1024]{1,0:T(8,128)(2,1)S(1)} %collective-permute-done.1.refs_2_), channel_id=1, source_target_pairs={{0,1},{1,0},{2,3},{3,2},{4,5},{5,4},{6,7},{7,6},{8,9},{9,8},{10,11... | collective-permute-start | bytes 245768 | tf_op jit(solution)/shard_map/ppermute | solution.py:340
  11.1 1.4 %collective-permute-start.4 = (bf16[40,1024]{1,0:T(8,128)(2,1)S(1)}, bf16[40,1024]{1,0:T(8,128)(2,1)S(1)}, u32[]{:S(2)}, u32[]{:S(2)}) collective-permute-start(bf16[40,1024]{1,0:T(8,128)(2,1)S(1)} %collective-permute-done.3.refs_4_), channel_id=1, source_target_pairs={{0,1},{1,0},{2,3},{3,2},{4,5},{5,4},{6,7},{7,6},{8,9},{9,8},{10,11... | collective-permute-start | bytes 245768 | tf_op jit(solution)/shard_map/ppermute | solution.py:340
  11.6 1.3 %collective-permute-start.6 = (bf16[40,1024]{1,0:T(8,128)(2,1)S(1)}, bf16[40,1024]{1,0:T(8,128)(2,1)S(1)}, u32[]{:S(2)}, u32[]{:S(2)}) collective-permute-start(bf16[40,1024]{1,0:T(8,128)(2,1)S(1)} %collective-permute-done.5.refs_6_), channel_id=1, source_target_pairs={{0,1},{1,0},{2,3},{3,2},{4,5},{5,4},{6,7},{7,6},{8,9},{9,8},{10,11... | collective-permute-start | bytes 245768 | tf_op jit(solution)/shard_map/ppermute | solution.py:340
  14.6 7.3 %collective-permute-start.12 = (bf16[64,1024]{1,0:T(8,128)(2,1)S(1)}, bf16[64,1024]{1,0:T(8,128)(2,1)S(1)}, u32[]{:S(2)}, u32[]{:S(2)}) collective-permute-start(bf16[64,1024]{1,0:T(8,128)(2,1)S(1)} %get-tuple-element.36.refs_0_), channel_id=1, source_target_pairs={{0,6},{1,7},{2,4},{3,5},{4,2},{5,3},{6,0},{7,1},{8,14},{9,15},{10,... | collective-permute-start | bytes 393224 | tf_op jit(solution)/shard_map/ppermute | solution.py:340
  16.3 7.7 %collective-permute-start.10 = (bf16[64,1024]{1,0:T(8,128)(2,1)S(1)}, bf16[64,1024]{1,0:T(8,128)(2,1)S(1)}, u32[]{:S(2)}, u32[]{:S(2)}) collective-permute-start(bf16[64,1024]{1,0:T(8,128)(2,1)S(1)} %get-tuple-element.36.refs_0_), channel_id=1, source_target_pairs={{0,4},{1,5},{2,6},{3,7},{4,0},{5,1},{6,2},{7,3},{8,12},{9,13},{10,... | collective-permute-start | bytes 393224 | tf_op jit(solution)/shard_map/ppermute | solution.py:340
  17.1 6.9 %collective-permute-start.8 = (bf16[64,1024]{1,0:T(8,128)(2,1)S(1)}, bf16[64,1024]{1,0:T(8,128)(2,1)S(1)}, u32[]{:S(2)}, u32[]{:S(2)}) collective-permute-start(bf16[64,1024]{1,0:T(8,128)(2,1)S(1)} %get-tuple-element.36.refs_0_), channel_id=1, source_target_pairs={{0,2},{1,3},{2,0},{3,1},{4,6},{5,7},{6,4},{7,5},{8,10},{9,11},{10,... | collective-permute-start | bytes 393224 | tf_op jit(solution)/shard_map/ppermute | solution.py:340
  18.2 8.0 %collective-permute-start.7 = (bf16[64,1024]{1,0:T(8,128)(2,1)S(1)}, bf16[64,1024]{1,0:T(8,128)(2,1)S(1)}, u32[]{:S(2)}, u32[]{:S(2)}) collective-permute-start(bf16[64,1024]{1,0:T(8,128)(2,1)S(1)} %get-tuple-element.36.refs_0_), channel_id=1, source_target_pairs={{0,1},{1,0},{2,3},{3,2},{4,5},{5,4},{6,7},{7,6},{8,9},{9,8},{10,11... | collective-permute-start | bytes 393224 | tf_op jit(solution)/shard_map/ppermute | solution.py:340
  24.1 4.7 %collective-permute-start.9 = (bf16[64,1024]{1,0:T(8,128)(2,1)S(1)}, bf16[64,1024]{1,0:T(8,128)(2,1)S(1)}, u32[]{:S(2)}, u32[]{:S(2)}) collective-permute-start(bf16[64,1024]{1,0:T(8,128)(2,1)S(1)} %collective-permute-done.8.refs_2_), channel_id=1, source_target_pairs={{0,1},{1,0},{2,3},{3,2},{4,5},{5,4},{6,7},{7,6},{8,9},{9,8},{10,11... | collective-permute-start | bytes 393224 | tf_op jit(solution)/shard_map/ppermute | solution.py:340
  24.1 5.0 %collective-permute-start.11 = (bf16[64,1024]{1,0:T(8,128)(2,1)S(1)}, bf16[64,1024]{1,0:T(8,128)(2,1)S(1)}, u32[]{:S(2)}, u32[]{:S(2)}) collective-permute-start(bf16[64,1024]{1,0:T(8,128)(2,1)S(1)} %collective-permute-done.10.refs_4_), channel_id=1, source_target_pairs={{0,1},{1,0},{2,3},{3,2},{4,5},{5,4},{6,7},{7,6},{8,9},{9,8},{10,11... | collective-permute-start | bytes 393224 | tf_op jit(solution)/shard_map/ppermute | solution.py:340
  24.6 4.4 %collective-permute-start.13 = (bf16[64,1024]{1,0:T(8,128)(2,1)S(1)}, bf16[64,1024]{1,0:T(8,128)(2,1)S(1)}, u32[]{:S(2)}, u32[]{:S(2)}) collective-permute-start(bf16[64,1024]{1,0:T(8,128)(2,1)S(1)} %collective-permute-done.12.refs_6_), channel_id=1, source_target_pairs={{0,1},{1,0},{2,3},{3,2},{4,5},{5,4},{6,7},{7,6},{8,9},{9,8},{10,11... | collective-permute-start | bytes 393224 | tf_op jit(solution)/shard_map/ppermute | solution.py:340
  24.6 13.4 %collective-permute-start.14 = (bf16[144,256]{1,0:T(8,128)(2,1)S(1)}, bf16[144,256]{1,0:T(8,128)(2,1)S(1)}, u32[]{:S(2)}, u32[]{:S(2)}) collective-permute-start(bf16[144,256]{1,0:T(8,128)(2,1)S(1)} %get-tuple-element.47), channel_id=1, source_target_pairs={{0,8},{8,0},{16,24},{24,16},{1,9},{9,1},{17,25},{25,17},{2,10},{10... | collective-permute-start | bytes 221192 | tf_op jit(solution)/shard_map/ppermute | solution.py:340
  26.1 11.9 %collective-permute-start.15 = (bf16[144,256]{1,0:T(8,128)(2,1)S(1)}, bf16[144,256]{1,0:T(8,128)(2,1)S(1)}, u32[]{:S(2)}, u32[]{:S(2)}) collective-permute-start(bf16[144,256]{1,0:T(8,128)(2,1)S(1)} %get-tuple-element.48), channel_id=1, source_target_pairs={{0,16},{8,24},{16,0},{24,8},{1,17},{9,25},{17,1},{25,9},{2,18},{10... | collective-permute-start | bytes 221192 | tf_op jit(solution)/shard_map/ppermute | solution.py:340
  28.7 9.3 %collective-permute-start.16 = (bf16[144,256]{1,0:T(8,128)(2,1)S(1)}, bf16[144,256]{1,0:T(8,128)(2,1)S(1)}, u32[]{:S(2)}, u32[]{:S(2)}) collective-permute-start(bf16[144,256]{1,0:T(8,128)(2,1)S(1)} %get-tuple-element.49), channel_id=1, source_target_pairs={{0,24},{8,16},{16,8},{24,0},{1,25},{9,17},{17,9},{25,1},{2,26},{10... | collective-permute-start | bytes 221192 | tf_op jit(solution)/shard_map/ppermute | solution.py:340
  33.0 12.4 %all-to-all-start = ((f32[32,4,128]{2,1,0:T(4,128)}), f32[32,4,128]{2,1,0:T(4,128)S(1)}, u32[]{:S(2)}, u32[]{:S(2)}) async-start(f32[32,4,128]{2,1,0:T(4,128)} %shard_map.64), calls=%async_computation | async-start | bytes 131072 | tf_op jit(solution)/shard_map/all_to_all | solution.py:429
  38.0 0.6 %copy-start = (bf16[144,256]{1,0:T(8,128)(2,1)}, bf16[144,256]{1,0:T(8,128)(2,1)S(1)}, u32[]{:S(2)}) copy-start(bf16[144,256]{1,0:T(8,128)(2,1)S(1)} %collective-permute-done.14.refs_1_) | copy-start | bytes 221188
  38.0 0.6 %copy-start.1 = (bf16[144,256]{1,0:T(8,128)(2,1)}, bf16[144,256]{1,0:T(8,128)(2,1)S(1)}, u32[]{:S(2)}) copy-start(bf16[144,256]{1,0:T(8,128)(2,1)S(1)} %collective-permute-done.15.refs_2_) | copy-start | bytes 221188
  38.7 0.6 %copy-start.2 = (bf16[144,256]{1,0:T(8,128)(2,1)}, bf16[144,256]{1,0:T(8,128)(2,1)S(1)}, u32[]{:S(2)}) copy-start(bf16[144,256]{1,0:T(8,128)(2,1)S(1)} %collective-permute-done.16.refs_3_) | copy-start | bytes 221188

commit v3 on v2

--- a/solution.py
+++ b/solution.py
@@ -32,6 +32,10 @@
 
 def as_bf(mask):
     return jnp.where(mask, 1.0, 0.0).astype(BF)
+
+
+def here():
+    return lax.axis_index("cent"), lax.axis_index("dp")
 
 
 def call(kernel, outs, args, us=0.0, scratch=(), smem=0, hbm_in=(), hbm_out=(), vmem_in=(), vmem_out=()):
@@ -62,7 +66,7 @@
     )(*args)
 
 
-def pack_kernel(me_ref, x_ref, prim_ref, sec_ref, out_ref, ids_ref, sems):
+def pack_kernel(x_ref, prim_ref, sec_ref, out_ref, ids_ref, sems):
     rows = x_ref.shape[0]
     copies = [
         pltpu.make_async_copy(prim_ref, ids_ref.at[pl.ds(0, 1)], sems.at[0]),
@@ -98,37 +102,36 @@
         copy.wait()
 
 
-def rows_kernel(rows, cap, parts, shift, me_ref, *refs):
+def slots_of(ids, rows, cap, parts, shift):
+    group = rows * parts
+    row, lane = iota((group, group), 0), iota((group, group), 1)
+    before = as_bf((row < lane) & (row // rows == lane // rows))
+    same = iota((parts, group), 0) == (ids >> shift)
+    count = nn(as_bf(same), before)
+    rank = jnp.sum(jnp.where(same, count, 0.0), axis=0, keepdims=True).astype(I32)
+    return (iota((1, group), 1) // rows) * cap + rank
+
+
+def rows_kernel(rows, cap, parts, shift, *refs):
     blocks = refs[:parts]
     cent_ref, info_ref, out_ref = refs[parts:]
     group = rows * parts
-    me = me_ref[0]
+    me, me_dp = here()
     spread = as_bf(iota((128, group), 0) == (iota((128, group), 1) % rows))
     lane_block = iota((META, group), 1) // rows
+    got = nn(jnp.concatenate([ref[rows : rows + META, 0:128] for ref in blocks], axis=0), spread)
     bytes8 = jnp.zeros((META, group), F32)
-    for s, ref in enumerate(blocks):
-        got = nn(ref[rows : rows + META, 0:128], spread)
-        bytes8 = bytes8 + jnp.where(lane_block == (me ^ s), got, 0.0)
+    for s in range(parts):
+        at = slice(s * META, (s + 1) * META)
+        bytes8 = bytes8 + jnp.where(lane_block == (me ^ s), got[at, :], 0.0)
     bytes8 = bytes8.astype(I32)
     prim = bytes8[0:1] * 256 + bytes8[1:2]
     sec = bytes8[2:3] * 256 + bytes8[3:4]
-    before = (iota((group, group), 0) < iota((group, group), 1)) & (
-        iota((group, group), 0) // rows == iota((group, group), 1) // rows
-    )
-    before = as_bf(before)
-    ranks = []
-    for ids in (prim, sec):
-        same = iota((parts, group), 0) == (ids >> shift)
-        count = nn(as_bf(same), before)
-        ranks.append(jnp.sum(jnp.where(same, count, 0.0), axis=0, keepdims=True).astype(I32))
-    base = (iota((1, group), 1) // rows) * cap
-    slot_p = base + ranks[0]
-    slot_s = base + ranks[1]
+    slot_p = slots_of(prim, rows, cap, parts, shift)
     info_ref[0:1, :] = prim
     info_ref[1:2, :] = sec
     info_ref[2:3, :] = slot_p
-    info_ref[3:4, :] = slot_s
-    info_ref[4:8, :] = jnp.zeros((4, group), I32)
+    info_ref[3:8, :] = jnp.zeros((5, group), I32)
     slots = cap * parts
     keep = (iota((slots, group), 0) == slot_p) & ((prim >> shift) == me)
     local = jnp.where(keep, (prim & ((1 << shift) - 1)) + 1, 0).astype(F32)
@@ -137,20 +140,18 @@
     out_ref[...] = nn(pick, cent_ref[...]).astype(BF)
 
 
-def slots_kernel(rows, cap, parts, dps, shift, me_ref, *refs):
+def slots_kernel(rows, cap, parts, dps, shift, *refs):
     blocks = refs[:parts]
     info_ref, x_ref = refs[parts : parts + 2]
-    outs = refs[parts + 2 : parts + 2 + dps]
-    picked_ref = refs[-1]
+    out_ref, picked_ref = refs[parts + 2 :]
     group = rows * parts
     slots = cap * parts
-    me = me_ref[0]
-    me_dp = me_ref[1]
+    me, me_dp = here()
     for s, ref in enumerate(blocks):
         at = pl.multiple_of((me ^ s) * rows, rows)
         x_ref[pl.ds(at, rows), :] = ref[0:rows, :]
     prim, sec = info_ref[0:1, :], info_ref[1:2, :]
-    slot_p, slot_s = info_ref[2:3, :], info_ref[3:4, :]
+    slot_p, slot_s = info_ref[2:3, :], slots_of(sec, rows, cap, parts, shift)
     keep_p = (iota((slots, group), 0) == slot_p) & ((prim >> shift) == me)
     keep_s = (iota((slots, group), 0) == slot_s) & ((sec >> shift) == me)
     pick = jnp.concatenate([as_bf(keep_p), as_bf(keep_s)], axis=0)
@@ -180,9 +181,8 @@
     facts = jnp.concatenate([nt(meta, pick), nt(loc, pick)], axis=0).astype(BF)
     width = x_ref.shape[1] // dps
     for s in range(dps):
-        at = pl.multiple_of((me_dp ^ s) * width, width)
-        outs[s][0 : 2 * slots, :] = picked_ref[:, pl.ds(at, width)]
-        outs[s][2 * slots :, 0:128] = facts
+        out_ref[s, 0 : 2 * slots, :] = picked_ref[:, s * width : (s + 1) * width]
+        out_ref[s, 2 * slots :, 0:128] = facts
 
 
 def base_kernel(tile, x_ref, cent_ref, out_ref, token_ref):
@@ -194,12 +194,12 @@
     token_ref[...] = jnp.zeros(token_ref.shape, F32)
 
 
-def score_kernel(rows, cap, parts, shift, tile, me_ref, *refs):
+def score_kernel(rows, cap, parts, shift, tile, *refs):
     owned = refs[:parts]
     x_ref, info_ref, cent_ref, base_ref, out_ref, r_ref, t_ref = refs[parts:]
     group = rows * parts
     slots = cap * parts
-    me = me_ref[0]
+    me, me_dp = here()
     dim = x_ref.shape[1]
     prim, sec, slot_p = info_ref[0:1, :], info_ref[1:2, :], info_ref[2:3, :]
     place = ((prim >> shift) ^ me) * slots + slot_p
@@ -244,26 +244,20 @@
     return high, (a - high.astype(F32)).astype(BF)
 
 
-def lists_kernel(cap, parts, dps, shift, group, tile, me_ref, *refs):
-    blocks = refs[:dps]
-    cent_ref, sum_ref, diff_ref, ids_ref, lane_ref, c_ref, blocks_ref, sems = refs[dps:]
+def lists_kernel(cap, parts, dps, shift, group, tile, *refs):
+    blocks_ref, cent_ref, sum_ref, diff_ref, ids_ref, lane_ref, c_ref, sem = refs
+    blocks = [blocks_ref.at[s] for s in range(dps)]
     slots = cap * parts
     cents = 1 << shift
     width = blocks[0].shape[1]
-    at = pl.multiple_of(me_ref[1] * width, width)
-    copies = [pltpu.make_async_copy(cent_ref.at[:, pl.ds(at, width)], c_ref, sems.at[0])]
-    for s in range(1, dps):
-        copies.append(pltpu.make_async_copy(blocks[s], blocks_ref.at[s - 1], sems.at[s]))
-    for copy in copies:
-        copy.start()
-    for copy in copies:
-        copy.wait()
-    diffs, ids_p, ids_s = [], [], []
-    for s in range(dps):
-        ref = blocks_ref.at[s - 1] if s else blocks[0]
+    at = pl.multiple_of(here()[1] * width, width)
+    copy = pltpu.make_async_copy(cent_ref.at[:, pl.ds(at, width)], c_ref, sem)
+    copy.start()
+    picks, ids_p, ids_s = [], [], []
+    second = iota((1, 128), 1) >= slots
+    for s, ref in enumerate(blocks):
         facts = ref[2 * slots :, 0:128].astype(F32)
         valid = facts[0:1, :] > 0.0
-        second = iota((1, 128), 1) >= slots
         high = jnp.where(second, facts[10:11, :], facts[8:9, :])
         low = jnp.where(second, facts[11:12, :], facts[9:10, :])
         ids = jnp.where(valid, high * 256.0 + low, -1.0)
@@ -272,31 +266,29 @@
         ids_s.append(ids[:, slots : 2 * slots])
         ids_col = jnp.transpose(jnp.broadcast_to(ids, (128, 128)))[:, 0:1].astype(I32)
         where_col = jnp.transpose(jnp.broadcast_to(where, (128, 128)))[slots:, 0:1].astype(I32)
-        lane_ref[s * slots : (s + 1) * slots, :] = as_bf(
-            iota((slots, group), 1) == where_col
-        )
-        pick = as_bf(iota((128, cents), 1) == ids_col)
-        rows = nn(pick, c_ref[...])
-        diff = ref[0 : 2 * slots, :].astype(F32) - rows
+        lane_ref[s * slots : (s + 1) * slots, :] = as_bf(iota((slots, group), 1) == where_col)
+        picks.append(as_bf(iota((128, cents), 1) == ids_col))
+    ids_p = jnp.concatenate(ids_p, axis=1).astype(I32)
+    ids_s = jnp.concatenate(ids_s, axis=1).astype(I32)
+    ids_ref[...] = jnp.broadcast_to(ids_s, ids_ref.shape)
+    copy.wait()
+    rows = nn(jnp.concatenate(picks, axis=0), c_ref[...])
+    diffs = []
+    for s, ref in enumerate(blocks):
+        diff = ref[0 : 2 * slots, :].astype(F32) - rows[s * 128 : (s + 1) * 128, :]
         diff_ref[s * slots : (s + 1) * slots, :] = diff[slots:, :]
         diffs.append(diff[0:slots, :])
     high, low = split(jnp.concatenate(diffs, axis=0))
-    ids_p = jnp.concatenate(ids_p, axis=1).astype(I32)
-    ids_s = jnp.concatenate(ids_s, axis=1).astype(I32)
-    ids_ref[...] = jnp.broadcast_to(ids_s, ids_ref.shape)
-
-    @pl.loop(0, cents, step=tile)
-    def _(k):
-        k = pl.multiple_of(k, tile)
+    for k in range(0, cents, tile):
         hot = as_bf((iota((tile, dps * slots), 0) + k) == ids_p)
-        sum_ref[pl.ds(k, tile), :] = nn(hot, high) + nn(hot, low)
-
-
-def final_kernel(rows, cap, parts, dps, group, tile, log_count, me_ref, *refs):
+        sum_ref[k : k + tile, :] = nn(hot, high) + nn(hot, low)
+
+
+def final_kernel(rows, cap, parts, dps, group, tile, log_count, *refs):
     got_ref, sum_ref, diff_ref, ids_ref, lane_ref, cost_ref, out_ref, weight_ref, part_ref, sems = refs
     slots = cap * parts
     lines = group // 128
-    me = me_ref[0]
+    me, me_dp = here()
     part = got_ref[:, 0:lines, :].reshape(dps, parts, lines, 128)
     top = jnp.max(part, axis=1)
     lse = top + jnp.log(jnp.sum(jnp.exp(part - top[:, None]), axis=1))
@@ -314,7 +306,7 @@
     terms = []
     for s in range(dps):
         at = slice(s * slots, (s + 1) * slots)
-        mine = weight_ref[pl.ds(me_ref[1] ^ s, 1), :]
+        mine = weight_ref[s : s + 1, :]
         column = jnp.sum(lane_ref[at, :].astype(F32) * mine, axis=1, keepdims=True)
         terms.append(column * diff_ref[at, :])
     high, low = split(jnp.concatenate(terms, axis=0))
@@ -327,7 +319,7 @@
         part_ref[at, :] = (sum_ref[at, :] + (nn(hot, high) + nn(hot, low))).astype(BF)
         copies.append(pltpu.make_async_copy(part_ref.at[at], out_ref.at[at], sems.at[i]))
         copies[i].start()
-    flat = weight_ref[pl.ds(dps + me_ref[1], 1), :]
+    flat = weight_ref[pl.ds(dps + me_dp, 1), :]
     cost = jnp.zeros((1, rows), F32)
     for b in range(parts):
         cost = cost + jnp.where(me == b, flat[:, b * rows : (b + 1) * rows], 0.0)
@@ -349,8 +341,7 @@
 
 
 def all_blocks(far, token, count):
-    near = [swap(far[0], "cent", count, 1)]
-    near += [swap(after(a, token), "cent", count, 1) for a in far[1:]]
+    near = [swap(after(a, token), "cent", count, 1) for a in far]
     return [a for pair in zip(far, near) for a in pair]
 
 
@@ -368,14 +359,12 @@
     tile = 256
     lines = group // 128
     token_out = ((8, 128), F32)
-    me = jnp.stack([lax.axis_index("cent"), lax.axis_index("dp")]).astype(I32)
 
     (packed,) = call(
         pack_kernel,
         [((rows + META, dim), BF)],
-        [me, vectors, primary.reshape(1, rows), secondary.reshape(1, rows)],
-        smem=1,
-        hbm_in=(1, 2, 3),
+        [vectors, primary.reshape(1, rows), secondary.reshape(1, rows)],
+        hbm_in=(0, 1, 2),
         scratch=[pltpu.VMEM((2, rows), I32), pltpu.SemaphoreType.DMA((3,))],
     )
     packed, cent = lax.optimization_barrier((packed, centroids))
@@ -393,21 +382,19 @@
     info, owned = call(
         functools.partial(rows_kernel, rows, cap, parts, shift),
         [((8, group), I32), ((slots, dim), BF)],
-        [me, *blocks, cent],
+        [*blocks, cent],
         us=2.0,
-        smem=1,
-        vmem_in=(parts + 1,),
+        vmem_in=(parts,),
     )
     far = far_blocks(owned, parts)
-    x_all, *columns = call(
+    x_all, columns = call(
         functools.partial(slots_kernel, rows, cap, parts, dps, shift),
-        [((group, dim), BF)] + [((2 * slots + 16, width), BF)] * dps,
-        [me, *blocks, info],
+        [((group, dim), BF), ((dps, 2 * slots + 16, width), BF)],
+        [*blocks, info],
         us=1.0,
-        smem=1,
         scratch=[pltpu.VMEM((2 * slots, dim), BF)],
     )
-    columns = [columns[0]] + [swap(columns[s], "dp", dps, s) for s in range(1, dps)]
+    columns = lax.all_to_all(columns, "dp", 0, 0, tiled=True)
     base, token = call(
         functools.partial(base_kernel, tile),
         [((cents, group), F32), token_out],
@@ -416,16 +403,16 @@
         vmem_in=(1,),
     )
     owned = all_blocks(far, token, parts)
+    owned[0], columns = lax.optimization_barrier((owned[0], columns))
     (sent,) = call(
         functools.partial(score_kernel, rows, cap, parts, shift, tile),
         [((dps * parts, 2 * lines, 128), F32)],
-        [me, *owned, x_all, info, cent, base],
+        [*owned, x_all, info, cent, base],
         us=6.0,
-        smem=1,
-        vmem_in=(parts + 3,),
+        vmem_in=(parts + 2,),
         scratch=[pltpu.VMEM((group, dim), BF), pltpu.VMEM((cents, group), F32)],
     )
-    sent, columns[0] = lax.optimization_barrier((sent, columns[0]))
+    columns = after(columns, sent)
     got = lax.all_to_all(sent, ("dp", "cent"), 0, 0, tiled=True)
     list_sum, diff, ids, lane = call(
         functools.partial(lists_kernel, cap, parts, dps, shift, group, tile),
@@ -435,22 +422,20 @@
             ((8, dps * slots), I32),
             ((dps * slots, group), BF),
         ],
-        [me, *columns, centroids],
-        smem=1,
-        hbm_in=tuple(range(2, dps + 2)),
+        [columns, centroids],
+        hbm_in=(1,),
+        vmem_in=(0,),
         us=4.0,
         scratch=[
             pltpu.VMEM((cents, width), BF),
-            pltpu.VMEM((dps - 1, 2 * slots + 16, width), BF),
-            pltpu.SemaphoreType.DMA((dps,)),
+            pltpu.SemaphoreType.DMA,
         ],
     )
     log_count = math.log(cents * parts)
     cost, out = call(
         functools.partial(final_kernel, rows, cap, parts, dps, group, tile, log_count),
         [((1, rows), F32), ((cents, width), BF)],
-        [me, got, list_sum, diff, ids, lane],
-        smem=1,
+        [got, list_sum, diff, ids, lane],
         hbm_out=(1,),
         scratch=[
             pltpu.VMEM((2 * dps, group), F32),

time: 48.3 us -> 54.8 us (1.13)
  local copies, waits for them, and re-layouts: 1.26 us -> 9.27 us
  Pallas kernels: 20 us -> 17.1 us
  starting transfers between devices: 18.7 us -> 19.7 us
    unnamed x6 -> x10, local copies, waits for them, and re-layouts: 1.26 us -> 9.27 us
    all_to_all x0 -> x1, starting transfers between devices: none -> 4.87 us  [per_device(): columns = lax.all_to_all(columns, 'dp', 0, 0, tiled=True)]
    ppermute x17 -> x14, starting transfers between devices: 13.6 us -> 9.6 us  [swap(): return lax.ppermute(a, axis, [(i, i ^ step) for i in range(count)])]
    pallas_call x8, Pallas kernels: 20 us -> 17.1 us  [call(): pl.pallas_call(kernel, out_shape=tuple((pltpu.VMEM(s, t) if i in vmem_out...]
    all_to_all x1, waiting for transfers between devices: 1.51 us -> 3.73 us  [per_device(): got = lax.all_to_all(sent, ('dp', 'cent'), 0, 0, tiled=True)]
    ppermute x17 -> x14, waiting for transfers between devices: 5.8 us -> 3.89 us  [swap(): return lax.ppermute(a, axis, [(i, i ^ step) for i in range(count)])]
  transfers between devices with their start and end apart: 18 -> 16, of which waited for: 9 -> 12; matrix products, arithmetic and copies ran while one was open for 0% -> 0% of each run, Pallas kernels for 29% -> 15%
where the time goes in v3:
time: 54.8 us; the launch traced here: 54.4 us
  starting transfers between devices  19.7 us (36%)
  Pallas kernels  17.1 us (31%)
  local copies, waits for them, and re-layouts  9.27 us (17%)
  waiting for transfers between devices  7.63 us (14%)
  between operations  0.7 us (1%)
    pallas_call x8, Pallas kernels, call(): pl.pallas_call(kernel, out_shape=tuple((pltpu.VMEM(s, t) if i in vmem_out...  17.1 us
    ppermute x14, starting transfers between devices, swap(): return lax.ppermute(a, axis, [(i, i ^ step) for i in range(count)])  9.6 us
    unnamed x10, local copies, waits for them, and re-layouts  9.27 us
    all_to_all x1, starting transfers between devices, per_device(): got = lax.all_to_all(sent, ('dp', 'cent'), 0, 0, tiled=True)  5.28 us
    all_to_all x1, starting transfers between devices, per_device(): columns = lax.all_to_all(columns, 'dp', 0, 0, tiled=True)  4.87 us
    ppermute x14, waiting for transfers between devices, swap(): return lax.ppermute(a, axis, [(i, i ^ step) for i in range(count)])  3.89 us
    all_to_all x1, waiting for transfers between devices, per_device(): got = lax.all_to_all(sent, ('dp', 'cent'), 0, 0, tiled=True)  3.73 us
  transfers between devices with their start and end apart: 16, of which 12 were waited for; matrix products, arithmetic and copies ran while one was open for 0% of the time, Pallas kernels for 15%

profile of v3, /device:TPU:0, one launch (start us, length us, event | category | flops | bytes accessed | tf_op | source)
XLA Modules:
  0.0 54.4 jit_solution(2005391437529995533)
XLA Ops:
  0.6 0.9 %shard_map.59.refs_0_ = bf16[40,1024]{1,0:T(8,128)(2,1)S(1)} custom-call(bf16[32,1024]{1,0:T(8,128)(2,1)} %x_ref.1, s32[1,32]{1,0:T(1,128)} %bitcast.3, s32[1,32]{1,0:T(1,128)} %bitcast.4), custom_call_target="tpu_custom_call" | custom-call | tf_op jit(solution)/shard_map/pallas_call | solution.py:50
  1.5 4.0 %collective-permute-start.5 = (bf16[40,1024]{1,0:T(8,128)(2,1)S(1)}, bf16[40,1024]{1,0:T(8,128)(2,1)S(1)}, u32[]{:S(2)}, u32[]{:S(2)}) collective-permute-start(bf16[40,1024]{1,0:T(8,128)(2,1)S(1)} %shard_map.59.refs_0_), channel_id=1, source_target_pairs={{0,6},{1,7},{2,4},{3,5},{4,2},{5,3},{6,0},{7,1},{8,14},{9,15},{10,... | collective-permute-start | bytes 245768 | tf_op jit(solution)/shard_map/ppermute | solution.py:332
  5.5 0.5 collective-permute-start.3
  6.0 0.1 collective-permute-start.1
  6.2 2.8 %shard_map.60 = (bf16[2048,1024]{1,0:T(8,128)(2,1)S(1)}, f32[8,128]{1,0:T(8,128)}) custom-call(bf16[2048,1024]{1,0:T(8,128)(2,1)} %refs_1_.1), custom_call_target="tpu_custom_call" | custom-call | flops 1500000000 | bytes 6000000 | tf_op jit(solution)/shard_map/pallas_call | solution.py:50
  9.0 0.1 collective-permute-start
  9.1 0.0 collective-permute-done.5.refs_6_
  9.1 0.9 %collective-permute-done.3.refs_4_ = bf16[40,1024]{1,0:T(8,128)(2,1)S(1)} collective-permute-done((bf16[40,1024]{1,0:T(8,128)(2,1)S(1)}, bf16[40,1024]{1,0:T(8,128)(2,1)S(1)}, u32[]{:S(2)}, u32[]{:S(2)}) %collective-permute-start.3) | collective-permute-done | bytes 81952 | tf_op jit(solution)/shard_map/ppermute | solution.py:332
  10.0 0.5 collective-permute-done.1.refs_2_
  10.5 0.0 collective-permute-start.2
  10.5 0.5 collective-permute-start.4
  11.0 0.0 collective-permute-start.6
  11.0 0.0 collective-permute-done.refs_1_
  11.0 0.8 %collective-permute-done.2.refs_3_ = bf16[40,1024]{1,0:T(8,128)(2,1)S(1)} collective-permute-done((bf16[40,1024]{1,0:T(8,128)(2,1)S(1)}, bf16[40,1024]{1,0:T(8,128)(2,1)S(1)}, u32[]{:S(2)}, u32[]{:S(2)}) %collective-permute-start.2) | collective-permute-done | bytes 81952 | tf_op jit(solution)/shard_map/ppermute | solution.py:332
  11.8 0.2 collective-permute-done.4.refs_5_
  11.9 0.4 collective-permute-done.6.refs_7_
  12.3 1.2 %shard_map.61 = (s32[8,256]{1,0:T(8,128)S(1)}, bf16[64,1024]{1,0:T(8,128)(2,1)S(1)}) custom-call(bf16[40,1024]{1,0:T(8,128)(2,1)S(1)} %shard_map.59.refs_0_, bf16[40,1024]{1,0:T(8,128)(2,1)S(1)} %collective-permute-done.refs_1_, bf16[40,1024]{1,0:T(8,128)(2,1)S(1)} %collective-permute-done.1.refs_2_, bf16[40,1024]{1,0:T(8,128)(2,1)S(1)} %collective-permute-done.2.refs_3_, ...), custom_call_target="tpu_custom_call" | custom-call | flops 1000000000 | bytes 4000000 | tf_op jit(solution)/shard_map/pallas_call | solution.py:50
  13.5 0.0 copy-start
  13.5 1.9 %copy-done = bf16[2048,1024]{1,0:T(8,128)(2,1)} copy-done((bf16[2048,1024]{1,0:T(8,128)(2,1)}, bf16[2048,1024]{1,0:T(8,128)(2,1)S(1)}, u32[]{:S(2)}) %copy-start) | copy-done | bytes 4194328
  15.4 1.1 %shard_map.62 = (bf16[256,1024]{1,0:T(8,128)(2,1)S(1)}, bf16[4,144,256]{2,1,0:T(8,128)(2,1)}) custom-call(bf16[40,1024]{1,0:T(8,128)(2,1)S(1)} %shard_map.59.refs_0_, bf16[40,1024]{1,0:T(8,128)(2,1)S(1)} %collective-permute-done.refs_1_, bf16[40,1024]{1,0:T(8,128)(2,1)S(1)} %collective-permute-done.1.refs_2_, ...), custom_call_target="tpu_custom_call" | custom-call | flops 500000000 | bytes 2000000 | tf_op jit(solution)/shard_map/pallas_call | solution.py:50
  16.5 4.9 %all-to-all-start = ((bf16[4,144,256]{2,1,0:T(8,128)(2,1)}), bf16[4,144,256]{2,1,0:T(8,128)(2,1)S(1)}, u32[]{:S(2)}, u32[]{:S(2)}) async-start(bf16[4,144,256]{2,1,0:T(8,128)(2,1)} %get-tuple-element.39), calls=%async_computation | async-start | bytes 589824 | tf_op jit(solution)/shard_map/all_to_all | solution.py:397
  21.4 1.7 %collective-permute-start.12 = (bf16[64,1024]{1,0:T(8,128)(2,1)S(1)}, bf16[64,1024]{1,0:T(8,128)(2,1)S(1)}, u32[]{:S(2)}, u32[]{:S(2)}) collective-permute-start(bf16[64,1024]{1,0:T(8,128)(2,1)S(1)} %get-tuple-element.43.refs_0_), channel_id=1, source_target_pairs={{0,6},{1,7},{2,4},{3,5},{4,2},{5,3},{6,0},{7,1},{8,14},{9,15},{10,... | collective-permute-start | bytes 393224 | tf_op jit(solution)/shard_map/ppermute | solution.py:332
  23.0 0.8 %collective-permute-start.10 = (bf16[64,1024]{1,0:T(8,128)(2,1)S(1)}, bf16[64,1024]{1,0:T(8,128)(2,1)S(1)}, u32[]{:S(2)}, u32[]{:S(2)}) collective-permute-start(bf16[64,1024]{1,0:T(8,128)(2,1)S(1)} %get-tuple-element.43.refs_0_), channel_id=1, source_target_pairs={{0,4},{1,5},{2,6},{3,7},{4,0},{5,1},{6,2},{7,3},{8,12},{9,13},{10,... | collective-permute-start | bytes 393224 | tf_op jit(solution)/shard_map/ppermute | solution.py:332
  23.8 1.0 %collective-permute-start.8 = (bf16[64,1024]{1,0:T(8,128)(2,1)S(1)}, bf16[64,1024]{1,0:T(8,128)(2,1)S(1)}, u32[]{:S(2)}, u32[]{:S(2)}) collective-permute-start(bf16[64,1024]{1,0:T(8,128)(2,1)S(1)} %get-tuple-element.43.refs_0_), channel_id=1, source_target_pairs={{0,2},{1,3},{2,0},{3,1},{4,6},{5,7},{6,4},{7,5},{8,10},{9,11},{10,... | collective-permute-start | bytes 393224 | tf_op jit(solution)/shard_map/ppermute | solution.py:332
  24.9 0.0 copy-start.1
  24.9 2.2 %copy-done.1 = bf16[2048,1024]{1,0:T(8,128)(2,1)S(1)} copy-done((bf16[2048,1024]{1,0:T(8,128)(2,1)S(1)}, bf16[2048,1024]{1,0:T(8,128)(2,1)}, u32[]{:S(2)}) %copy-start.1) | copy-done | bytes 4194328
  27.0 1.9 %shard_map.63 = (f32[2048,256]{1,0:T(8,128)S(1)}, f32[8,128]{1,0:T(8,128)}) custom-call(bf16[256,1024]{1,0:T(8,128)(2,1)S(1)} %get-tuple-element.41.x_ref.refs_8_, bf16[2048,1024]{1,0:T(8,128)(2,1)S(1)} %copy-done.1), custom_call_target="tpu_custom_call" | custom-call | flops 1000000000 | bytes 4000000 | tf_op jit(solution)/shard_map/pallas_call | solution.py:50
  28.9 0.0 copy-start.3
  28.9 1.3 %copy-done.3 = f32[2048,256]{1,0:T(8,128)} copy-done((f32[2048,256]{1,0:T(8,128)}, f32[2048,256]{1,0:T(8,128)S(1)}, u32[]{:S(2)}) %copy-start.3) | copy-done | bytes 2097176
  30.3 0.0 collective-permute-start.7
  30.3 0.0 collective-permute-done.12.refs_6_
  30.3 0.1 collective-permute-done.10.refs_4_
  30.4 0.1 collective-permute-done.8.refs_2_
  30.5 0.4 collective-permute-start.9
  30.8 0.1 collective-permute-start.11
  31.0 0.4 collective-permute-start.13
  31.4 0.0 all-to-all-done.refs_0_
  31.4 0.2 collective-permute-done.7.refs_1_
  31.6 0.2 collective-permute-done.9.refs_3_
  31.8 0.4 collective-permute-done.11.refs_5_
  32.2 0.2 collective-permute-done.13.refs_7_
  32.4 0.0 copy-start.2
  32.4 2.2 %copy-done.2 = bf16[2048,1024]{1,0:T(8,128)(2,1)S(1)} copy-done((bf16[2048,1024]{1,0:T(8,128)(2,1)S(1)}, bf16[2048,1024]{1,0:T(8,128)(2,1)}, u32[]{:S(2)}) %copy-start.2) | copy-done | bytes 4194328
  34.6 0.0 copy-start.4
  34.6 1.6 %copy-done.4 = f32[2048,256]{1,0:T(8,128)S(1)} copy-done((f32[2048,256]{1,0:T(8,128)S(1)}, f32[2048,256]{1,0:T(8,128)}, u32[]{:S(2)}) %copy-start.4) | copy-done | bytes 2097176
  36.2 3.4 %shard_map.64 = f32[32,4,128]{2,1,0:T(4,128)} custom-call(bf16[64,1024]{1,0:T(8,128)(2,1)S(1)} %get-tuple-element.43.refs_0_, bf16[64,1024]{1,0:T(8,128)(2,1)S(1)} %collective-permute-done.7.refs_1_, bf16[64,1024]{1,0:T(8,128)(2,1)S(1)} %collective-permute-done.8.refs_2_, bf16[64,1024]{1,0:T(8,128)(2,1)S(1)} %collective-permute-done.9.refs_3_, ...), custom_call_target="tpu_custom_call" | custom-call | flops 3000000000 | bytes 12000000 | tf_op jit(solution)/shard_map/pallas_call | solution.py:50
  39.6 5.3 %all-to-all-start.1 = ((f32[32,4,128]{2,1,0:T(4,128)}), f32[32,4,128]{2,1,0:T(4,128)S(1)}, u32[]{:S(2)}, u32[]{:S(2)}) async-start(f32[32,4,128]{2,1,0:T(4,128)} %shard_map.64), calls=%async_computation.1 | async-start | bytes 131072 | tf_op jit(solution)/shard_map/all_to_all | solution.py:416
  44.9 3.7 %shard_map.65 = (f32[2048,256]{1,0:T(8,128)S(1)}, f32[256,256]{1,0:T(8,128)S(1)}, s32[8,256]{1,0:T(8,128)S(1)}, bf16[256,256]{1,0:T(8,128)(2,1)S(1)}) custom-call(bf16[4,144,256]{2,1,0:T(8,128)(2,1)S(1)} %all-to-all-done.refs_0_, bf16[2048,1024]{1,0:T(8,128)(2,1)} %refs_1_.1), custom_call_target="tpu_custom_call" | custom-call | flops 2000000000 | bytes 8000000 | tf_op jit(solution)/shard_map/pallas_call | solution.py:50
  48.5 3.7 %all-to-all-done.1.refs_0_ = f32[32,4,128]{2,1,0:T(4,128)S(1)} async-done(((f32[32,4,128]{2,1,0:T(4,128)}), f32[32,4,128]{2,1,0:T(4,128)S(1)}, u32[]{:S(2)}, u32[]{:S(2)}) %all-to-all-start.1) | async-done | bytes 65568 | tf_op jit(solution)/shard_map/all_to_all | solution.py:416
  52.3 2.1 %shard_map.66 = (f32[1,32]{1,0:T(1,128)}, bf16[2048,256]{1,0:T(8,128)(2,1)}) custom-call(f32[32,4,128]{2,1,0:T(4,128)S(1)} %all-to-all-done.1.refs_0_, f32[2048,256]{1,0:T(8,128)S(1)} %get-tuple-element.50.refs_1_, f32[256,256]{1,0:T(8,128)S(1)} %get-tuple-element.51.refs_2_, s32[8,256]{1,0:T(8,128)S(1)} %get-tuple-element.52.refs_3_, ...), custom_call_target="tpu_custom_call" | custom-call | tf_op jit(solution)/shard_map/pallas_call | solution.py:50
Async XLA Ops:
  1.5 7.5 %collective-permute-start.5 = (bf16[40,1024]{1,0:T(8,128)(2,1)S(1)}, bf16[40,1024]{1,0:T(8,128)(2,1)S(1)}, u32[]{:S(2)}, u32[]{:S(2)}) collective-permute-start(bf16[40,1024]{1,0:T(8,128)(2,1)S(1)} %shard_map.59.refs_0_), channel_id=1, source_target_pairs={{0,6},{1,7},{2,4},{3,5},{4,2},{5,3},{6,0},{7,1},{8,14},{9,15},{10,... | collective-permute-start | bytes 245768 | tf_op jit(solution)/shard_map/ppermute | solution.py:332
  5.5 4.4 %collective-permute-start.3 = (bf16[40,1024]{1,0:T(8,128)(2,1)S(1)}, bf16[40,1024]{1,0:T(8,128)(2,1)S(1)}, u32[]{:S(2)}, u32[]{:S(2)}) collective-permute-start(bf16[40,1024]{1,0:T(8,128)(2,1)S(1)} %shard_map.59.refs_0_), channel_id=1, source_target_pairs={{0,4},{1,5},{2,6},{3,7},{4,0},{5,1},{6,2},{7,3},{8,12},{9,13},{10,... | collective-permute-start | bytes 245768 | tf_op jit(solution)/shard_map/ppermute | solution.py:332
  6.0 4.4 %collective-permute-start.1 = (bf16[40,1024]{1,0:T(8,128)(2,1)S(1)}, bf16[40,1024]{1,0:T(8,128)(2,1)S(1)}, u32[]{:S(2)}, u32[]{:S(2)}) collective-permute-start(bf16[40,1024]{1,0:T(8,128)(2,1)S(1)} %shard_map.59.refs_0_), channel_id=1, source_target_pairs={{0,2},{1,3},{2,0},{3,1},{4,6},{5,7},{6,4},{7,5},{8,10},{9,11},{10,... | collective-permute-start | bytes 245768 | tf_op jit(solution)/shard_map/ppermute | solution.py:332
  9.0 2.0 %collective-permute-start = (bf16[40,1024]{1,0:T(8,128)(2,1)S(1)}, bf16[40,1024]{1,0:T(8,128)(2,1)S(1)}, u32[]{:S(2)}, u32[]{:S(2)}) collective-permute-start(bf16[40,1024]{1,0:T(8,128)(2,1)S(1)} %shard_map.59.refs_0_), channel_id=1, source_target_pairs={{0,1},{1,0},{2,3},{3,2},{4,5},{5,4},{6,7},{7,6},{8,9},{9,8},{10,11... | collective-permute-start | bytes 245768 | tf_op jit(solution)/shard_map/ppermute | solution.py:332
  10.5 1.3 %collective-permute-start.2 = (bf16[40,1024]{1,0:T(8,128)(2,1)S(1)}, bf16[40,1024]{1,0:T(8,128)(2,1)S(1)}, u32[]{:S(2)}, u32[]{:S(2)}) collective-permute-start(bf16[40,1024]{1,0:T(8,128)(2,1)S(1)} %collective-permute-done.1.refs_2_), channel_id=1, source_target_pairs={{0,1},{1,0},{2,3},{3,2},{4,5},{5,4},{6,7},{7,6},{8,9},{9,8},{10,11... | collective-permute-start | bytes 245768 | tf_op jit(solution)/shard_map/ppermute | solution.py:332
  10.5 1.4 %collective-permute-start.4 = (bf16[40,1024]{1,0:T(8,128)(2,1)S(1)}, bf16[40,1024]{1,0:T(8,128)(2,1)S(1)}, u32[]{:S(2)}, u32[]{:S(2)}) collective-permute-start(bf16[40,1024]{1,0:T(8,128)(2,1)S(1)} %collective-permute-done.3.refs_4_), channel_id=1, source_target_pairs={{0,1},{1,0},{2,3},{3,2},{4,5},{5,4},{6,7},{7,6},{8,9},{9,8},{10,11... | collective-permute-start | bytes 245768 | tf_op jit(solution)/shard_map/ppermute | solution.py:332
  11.0 1.3 %collective-permute-start.6 = (bf16[40,1024]{1,0:T(8,128)(2,1)S(1)}, bf16[40,1024]{1,0:T(8,128)(2,1)S(1)}, u32[]{:S(2)}, u32[]{:S(2)}) collective-permute-start(bf16[40,1024]{1,0:T(8,128)(2,1)S(1)} %collective-permute-done.5.refs_6_), channel_id=1, source_target_pairs={{0,1},{1,0},{2,3},{3,2},{4,5},{5,4},{6,7},{7,6},{8,9},{9,8},{10,11... | collective-permute-start | bytes 245768 | tf_op jit(solution)/shard_map/ppermute | solution.py:332
  13.5 2.0 %copy-start = (bf16[2048,1024]{1,0:T(8,128)(2,1)}, bf16[2048,1024]{1,0:T(8,128)(2,1)S(1)}, u32[]{:S(2)}) copy-start(bf16[2048,1024]{1,0:T(8,128)(2,1)S(1)} %get-tuple-element.36.refs_8_.cent_ref.refs_10_) | copy-start | bytes 12582916
  16.5 14.9 %all-to-all-start = ((bf16[4,144,256]{2,1,0:T(8,128)(2,1)}), bf16[4,144,256]{2,1,0:T(8,128)(2,1)S(1)}, u32[]{:S(2)}, u32[]{:S(2)}) async-start(bf16[4,144,256]{2,1,0:T(8,128)(2,1)} %get-tuple-element.39), calls=%async_computation | async-start | bytes 589824 | tf_op jit(solution)/shard_map/all_to_all | solution.py:397
  21.4 8.9 %collective-permute-start.12 = (bf16[64,1024]{1,0:T(8,128)(2,1)S(1)}, bf16[64,1024]{1,0:T(8,128)(2,1)S(1)}, u32[]{:S(2)}, u32[]{:S(2)}) collective-permute-start(bf16[64,1024]{1,0:T(8,128)(2,1)S(1)} %get-tuple-element.43.refs_0_), channel_id=1, source_target_pairs={{0,6},{1,7},{2,4},{3,5},{4,2},{5,3},{6,0},{7,1},{8,14},{9,15},{10,... | collective-permute-start | bytes 393224 | tf_op jit(solution)/shard_map/ppermute | solution.py:332
  23.0 7.3 %collective-permute-start.10 = (bf16[64,1024]{1,0:T(8,128)(2,1)S(1)}, bf16[64,1024]{1,0:T(8,128)(2,1)S(1)}, u32[]{:S(2)}, u32[]{:S(2)}) collective-permute-start(bf16[64,1024]{1,0:T(8,128)(2,1)S(1)} %get-tuple-element.43.refs_0_), channel_id=1, source_target_pairs={{0,4},{1,5},{2,6},{3,7},{4,0},{5,1},{6,2},{7,3},{8,12},{9,13},{10,... | collective-permute-start | bytes 393224 | tf_op jit(solution)/shard_map/ppermute | solution.py:332
  23.8 6.6 %collective-permute-start.8 = (bf16[64,1024]{1,0:T(8,128)(2,1)S(1)}, bf16[64,1024]{1,0:T(8,128)(2,1)S(1)}, u32[]{:S(2)}, u32[]{:S(2)}) collective-permute-start(bf16[64,1024]{1,0:T(8,128)(2,1)S(1)} %get-tuple-element.43.refs_0_), channel_id=1, source_target_pairs={{0,2},{1,3},{2,0},{3,1},{4,6},{5,7},{6,4},{7,5},{8,10},{9,11},{10,... | collective-permute-start | bytes 393224 | tf_op jit(solution)/shard_map/ppermute | solution.py:332
  24.9 2.2 %copy-start.1 = (bf16[2048,1024]{1,0:T(8,128)(2,1)S(1)}, bf16[2048,1024]{1,0:T(8,128)(2,1)}, u32[]{:S(2)}) copy-start(bf16[2048,1024]{1,0:T(8,128)(2,1)} %copy-done) | copy-start | bytes 12582916
  28.9 1.4 %copy-start.3 = (f32[2048,256]{1,0:T(8,128)}, f32[2048,256]{1,0:T(8,128)S(1)}, u32[]{:S(2)}) copy-start(f32[2048,256]{1,0:T(8,128)S(1)} %get-tuple-element.47.refs_11_) | copy-start | bytes 6291460
  30.3 1.3 %collective-permute-start.7 = (bf16[64,1024]{1,0:T(8,128)(2,1)S(1)}, bf16[64,1024]{1,0:T(8,128)(2,1)S(1)}, u32[]{:S(2)}, u32[]{:S(2)}) collective-permute-start(bf16[64,1024]{1,0:T(8,128)(2,1)S(1)} %get-tuple-element.43.refs_0_), channel_id=1, source_target_pairs={{0,1},{1,0},{2,3},{3,2},{4,5},{5,4},{6,7},{7,6},{8,9},{9,8},{10,11... | collective-permute-start | bytes 393224 | tf_op jit(solution)/shard_map/ppermute | solution.py:332
  30.5 1.4 %collective-permute-start.9 = (bf16[64,1024]{1,0:T(8,128)(2,1)S(1)}, bf16[64,1024]{1,0:T(8,128)(2,1)S(1)}, u32[]{:S(2)}, u32[]{:S(2)}) collective-permute-start(bf16[64,1024]{1,0:T(8,128)(2,1)S(1)} %collective-permute-done.8.refs_2_), channel_id=1, source_target_pairs={{0,1},{1,0},{2,3},{3,2},{4,5},{5,4},{6,7},{7,6},{8,9},{9,8},{10,11... | collective-permute-start | bytes 393224 | tf_op jit(solution)/shard_map/ppermute | solution.py:332
  30.8 1.3 %collective-permute-start.11 = (bf16[64,1024]{1,0:T(8,128)(2,1)S(1)}, bf16[64,1024]{1,0:T(8,128)(2,1)S(1)}, u32[]{:S(2)}, u32[]{:S(2)}) collective-permute-start(bf16[64,1024]{1,0:T(8,128)(2,1)S(1)} %collective-permute-done.10.refs_4_), channel_id=1, source_target_pairs={{0,1},{1,0},{2,3},{3,2},{4,5},{5,4},{6,7},{7,6},{8,9},{9,8},{10,11... | collective-permute-start | bytes 393224 | tf_op jit(solution)/shard_map/ppermute | solution.py:332
  31.0 1.4 %collective-permute-start.13 = (bf16[64,1024]{1,0:T(8,128)(2,1)S(1)}, bf16[64,1024]{1,0:T(8,128)(2,1)S(1)}, u32[]{:S(2)}, u32[]{:S(2)}) collective-permute-start(bf16[64,1024]{1,0:T(8,128)(2,1)S(1)} %collective-permute-done.12.refs_6_), channel_id=1, source_target_pairs={{0,1},{1,0},{2,3},{3,2},{4,5},{5,4},{6,7},{7,6},{8,9},{9,8},{10,11... | collective-permute-start | bytes 393224 | tf_op jit(solution)/shard_map/ppermute | solution.py:332
  32.4 2.2 %copy-start.2 = (bf16[2048,1024]{1,0:T(8,128)(2,1)S(1)}, bf16[2048,1024]{1,0:T(8,128)(2,1)}, u32[]{:S(2)}) copy-start(bf16[2048,1024]{1,0:T(8,128)(2,1)} %copy-done) | copy-start | bytes 12582916
  34.6 1.6 %copy-start.4 = (f32[2048,256]{1,0:T(8,128)S(1)}, f32[2048,256]{1,0:T(8,128)}, u32[]{:S(2)}) copy-start(f32[2048,256]{1,0:T(8,128)} %copy-done.3) | copy-start | bytes 6291460
  39.6 12.7 %all-to-all-start.1 = ((f32[32,4,128]{2,1,0:T(4,128)}), f32[32,4,128]{2,1,0:T(4,128)S(1)}, u32[]{:S(2)}, u32[]{:S(2)}) async-start(f32[32,4,128]{2,1,0:T(4,128)} %shard_map.64), calls=%async_computation.1 | async-start | bytes 131072 | tf_op jit(solution)/shard_map/all_to_all | solution.py:416
